TPU v7x, 32 devices: a whole 2x2x4 slice. The times are simulated.
32 devices in a mesh: rows: 8 (over y, x, core), cols: 4 (over z).
Axes of the slice: x: 2, y: 2, z: 4, core: 2. Of those that a mesh axis runs over, the one named last changes fastest.
Arguments:
- panel: float32 [2048, 256], P(('rows', 'cols')), may hold values from -1 to 1, as said below
- trailing: float32 [2048, 2048], P('rows', 'cols'), may hold values from -6 to 6
Outputs:
- r_factor: float32 [256, 256], replicated
- coefficients: float32 [256, 2048], P(None, 'cols')
- updated: float32 [2048, 2048], P('rows', 'cols')
Inputs may be any that keep to these rules, and one draw needn't show every extreme that they name: panel has full column rank and is well conditioned; rows and columns carry different scales.
All inputs are finite; a program needn't handle non-finite values.
Results may differ from a plain program's by a relative error of at most 0.0003.
Values sent between devices are 32-bit elements; how exact they have to be, the bound alone decides.
No kernel may reach another device: no remote copies, remote signals or barrier semaphores. Data moves between devices by JAX's collectives and lax.ppermute only.
A program may use at most 64 MiB of HBM per device.

v0:
```python
import jax
import jax.numpy as jnp
from jax import lax
from jax.sharding import PartitionSpec as P


def product(left, right):
    return jnp.dot(left, right, precision=lax.Precision.HIGHEST)


def lower_inverse_of(lower):
    identity = jnp.eye(lower.shape[0], dtype=lower.dtype)
    return jax.scipy.linalg.solve_triangular(lower, identity, lower=True)


def cholesky_pair(matrix):
    lower = jnp.linalg.cholesky(matrix)
    return (lower, lower_inverse_of(lower))


def gram_of(matrix):
    return lax.dot_general(
        matrix, matrix, (((0,), (0,)), ((), ())), precision=lax.Precision.HIGHEST
    )


def cross_of(panel_block, trailing):
    return lax.dot_general(
        panel_block, trailing, (((0,), (0,)), ((), ())), precision=lax.Precision.HIGHEST
    )


def finish_early(lower_inverse, cross_terms, panel_block, trailing):
    coefficients = product(lower_inverse, cross_terms)
    mixing = product(lower_inverse.T, coefficients)
    updated = trailing - product(panel_block, mixing)
    return (coefficients, updated)


def local(panel, trailing):
    panel_block = lax.all_gather(panel, "cols", axis=0, tiled=True)
    width = panel_block.shape[1]
    stacked = jnp.concatenate([gram_of(panel_block), cross_of(panel_block, trailing)], axis=1)
    summed = lax.psum(stacked, "rows")
    lower, lower_inverse = cholesky_pair(summed[:, :width])
    r_upper = lower.T
    cross_joint = summed[:, width:]
    coefficients, updated = finish_early(lower_inverse, cross_joint, panel_block, trailing)
    return (r_upper, coefficients, updated)


def solution(mesh):
    return jax.shard_map(
        local,
        mesh=mesh,
        in_specs=(P(("rows", "cols"), None), P("rows", "cols")),
        out_specs=(P(), P(None, "cols"), P("rows", "cols")),
        check_vma=False,
    )
```

profile of v0, /device:TPU:0, one launch (start us, length us, event | category | flops | bytes accessed | tf_op | source)
XLA Modules:
  0.0 156.2 jit_solution(14104111784305048921)
XLA Ops:
  7.2 16.0 %all_gather.3 = f32[256,256]{1,0:T(8,128)S(1)} all-gather(f32[64,256]{1,0:T(8,128)} %param.2), channel_id=1, replica_groups=mesh['rows'=8,'cols'=4] {'cols'}, dimensions={0}, use_global_device_ids=true | all-gather | bytes 327680 | tf_op jit(solution)/shard_map/all_gather | solution.py:41
  23.2 0.6 fusion.17
  23.8 1.0 fusion.18
  24.8 1.0 pad_maximum_fusion
  26.1 57.1 %all-reduce.3.cloned.1.call-done = f32[256,768]{0,1:T(8,128)} async-done(((f32[256,768]{0,1:T(8,128)}), f32[256,768]{0,1:T(8,128)}) %all-reduce.3.cloned.1.call-update) | async-done | bytes 786448 | tf_op jit(solution)/shard_map/psum | solution.py:44
  83.2 0.9 slice-done
  84.5 11.7 %cholesky.50 = f32[128,128]{1,0:T(8,128)S(1)} custom-call(f32[128,128]{1,0:T(8,128)S(1)} %cholesky.118), custom_call_target="Cholesky" | custom-call | tf_op jit(solution)/shard_map/jit(cholesky)/cholesky | solution.py:17
  96.2 9.8 %custom-call.15 = f32[1,128,128]{1,2,0:T(8,128)S(1)} custom-call(f32[1,128,128]{2,1,0:T(8,128)S(1)} %get-tuple-element.29), custom_call_target="InvertDiagBlocksLowerTriangular" | custom-call | tf_op jit(solution)/shard_map/jit(cholesky)/cholesky | solution.py:17
  106.3 0.3 convolution_subtract_fusion.1
  106.5 11.9 %cholesky.105 = f32[128,128]{1,0:T(8,128)S(1)} custom-call(f32[128,128]{1,0:T(8,128)S(1)} %convolution_subtract_fusion.1), custom_call_target="Cholesky" | custom-call | tf_op jit(solution)/shard_map/jit(cholesky)/cholesky | solution.py:17
  118.5 0.6 compare_reduce_fusion
  120.5 4.0 %while.1 = (s32[]{:T(128)}, f32[256,256]{1,0:T(8,128)S(1)}, s32[2,2]{1,0:T(2,128)S(1)}, f32[2,128,128]{2,1,0:T(8,128)S(1)}, s32[]{:T(128)}) while((s32[]{:T(128)}, f32[256,256]{1,0:T(8,128)S(1)}, s32[2,2]{1,0:T(2,128)S(1)}, f32[2,128,128]{2,1,0:T(8,128)S(1)}, s32[]{:T(128)}) %tuple.29), condition=%wide.while_cond, body=%wide.while_body.sunk | while | flops 2 | bytes 131181 | solution.py:13
  120.5 0.6 fusion.31
  121.1 1.4 bitcast_dynamic-update-slice_fusion.2
  122.5 0.6 fusion.31
  123.1 1.4 bitcast_dynamic-update-slice_fusion.2
  124.5 19.7 %custom-call.16 = f32[2,128,128]{1,2,0:T(8,128)S(1)} custom-call(f32[2,128,128]{2,1,0:T(8,128)S(1)} %get-tuple-element.10), custom_call_target="InvertDiagBlocksLowerTriangular" | custom-call | tf_op jit(solution)/shard_map/jit(_solve_triangular)/triangular_solve | solution.py:13
  144.2 0.3 fusion.7
  144.7 0.3 fusion.10
  145.0 0.6 fusion.1
  145.7 0.6 fusion.6
  146.5 1.0 fusion
  147.5 1.0 copy.9
  148.5 0.8 copy.8
  (25 shorter events, 1.4 us)
Async XLA Ops:
  7.2 16.7 %copy-start = (f32[256,512]{1,0:T(8,128)S(1)}, f32[256,512]{1,0:T(8,128)}, u32[]{:S(2)}) copy-start(f32[256,512]{1,0:T(8,128)} %param.3) | copy-start | bytes 1572868
  7.2 76.0 %all-reduce.3.cloned.1.call-start = ((), (), s32[]{:S(2)}) async-start(), calls=%async_computation | async-start | bytes 1572864 | tf_op jit(solution)/shard_map/psum | solution.py:44
  83.2 0.9 slice-start
  83.2 1.2 copy-start.2
  145.7 0.8 copy-start.1
Sparse Core Ops, SparseCore 0:
  25.9 57.1 all-reduce.2
where the time goes:
time: 156 us
  waiting for transfers between devices  57.1 us (37%)
  other arithmetic  54.9 us (35%)
  blocking collectives  16 us (10%)
  between operations  15.5 us (10%)
  local copies, waits for them, and re-layouts  7.43 us (5%)
  matrix products  5.19 us (3%)
    psum x1, waiting for transfers between devices, local(): summed = lax.psum(stacked, 'rows')  57.1 us
    another operation x6, other arithmetic, cholesky_pair(): lower = jnp.linalg.cholesky(matrix)  34.1 us
    another operation x3, other arithmetic, lower_inverse_of(): return jax.scipy.linalg.solve_triangular(lower, identity, lower=True)  19.7 us
    all_gather x1, blocking collectives, local(): panel_block = lax.all_gather(panel, 'cols', axis=0, tiled=True)  16 us
    another operation x6, local copies, waits for them, and re-layouts  3.95 us
  transfers between devices with their start and end apart: 1, of which 1 were waited for; matrix products, arithmetic and copies ran while one was open for 0% of the time, Pallas kernels for 0%

commit v1 on v0

v1 whole, which is shorter than its diff:
```python
import functools

import jax
import jax.numpy as jnp
from jax import lax
from jax.experimental import pallas as pl
from jax.experimental.pallas import tpu as pltpu
from jax.sharding import PartitionSpec as P

LANES, SUBLANES, BLOCK = 128, 8, 32


def split(x):
    high = x.astype(jnp.bfloat16)
    return high, (x - high.astype(jnp.float32)).astype(jnp.bfloat16)


def product(left, right, over_left, over_right):
    lh, ll = split(left)
    rh, rl = split(right)
    return lax.dot_general(
        jnp.concatenate([lh, lh, ll], axis=over_left),
        jnp.concatenate([rh, rl, rh], axis=over_right),
        (((over_left,), (over_right,)), ((), ())),
        preferred_element_type=jnp.float32,
    )


def call(body, outs, *args, scratch=(), name=None, in_specs=None, out_specs=None):
    shapes = [jax.ShapeDtypeStruct(s, jnp.float32) for s in outs]
    extra = {}
    if in_specs is not None:
        extra["in_specs"] = in_specs
    if out_specs is not None:
        extra["out_specs"] = out_specs
    return pl.pallas_call(body, out_shape=shapes, scratch_shapes=list(scratch), name=name, **extra)(*args)


def gram_kernel(*refs, count):
    pieces, (panel_ref, keep_ref, send_ref) = refs[:count], refs[count:]
    height, width = pieces[0].shape
    half = width // 2
    here = lax.axis_index("cols")
    for step in range(count):
        at = lax.rem(here - step + count, count)
        panel_ref[pl.ds(pl.multiple_of(at * height, height), height), :] = pieces[step][...]
    block = panel_ref[...]
    gram = product(block, block, 0, 0)
    row = lax.broadcasted_iota(jnp.int32, (half, half), 0)
    col = lax.broadcasted_iota(jnp.int32, (half, half), 1)
    first, cross, second = gram[:half, :half], gram[:half, half:], gram[half:, half:]
    square = jnp.where(row > col, first, second)
    spare = jnp.sum(jnp.where(row == col, first, 0.0), axis=0, keepdims=True)
    spare = jnp.broadcast_to(spare, (SUBLANES, half))
    even = lax.rem(lax.axis_index("rows"), 2) == 0

    @pl.when(even)
    def _():
        keep_ref[:half, :] = cross
        keep_ref[half:, :] = jnp.zeros((SUBLANES, half), jnp.float32)
        send_ref[:half, :] = square
        send_ref[half:, :] = spare

    @pl.when(jnp.logical_not(even))
    def _():
        send_ref[:half, :] = cross
        send_ref[half:, :] = jnp.zeros((SUBLANES, half), jnp.float32)
        keep_ref[:half, :] = square
        keep_ref[half:, :] = spare


def unpack(mine_ref, other_ref, m_ref):
    width = m_ref.shape[0]
    half = width // 2
    even = lax.rem(lax.axis_index("rows"), 2) == 0

    def place(cross_ref, square_ref):
        square = square_ref[:half, :]
        spare = square_ref[half : half + 1, :]
        row = lax.broadcasted_iota(jnp.int32, (half, half), 0)
        col = lax.broadcasted_iota(jnp.int32, (half, half), 1)
        turned = square.T
        m_ref[:half, :half] = jnp.where(row > col, square, jnp.where(row < col, turned, spare))
        m_ref[half:, half:] = jnp.where(row <= col, square, turned)
        m_ref[:half, half:] = cross_ref[:half, :]
        m_ref[half:, :half] = jnp.zeros((half, half), jnp.float32)

    pl.when(even)(functools.partial(place, mine_ref, other_ref))
    pl.when(jnp.logical_not(even))(functools.partial(place, other_ref, mine_ref))


def along_sublanes(x, r):
    return jnp.broadcast_to(x[r : r + 1, :], x.shape)


def along_lanes(x, c):
    return jnp.broadcast_to(x[:, c : c + 1], (x.shape[0], LANES))


def factor_rows(rows, unit, tile, lane0):
    groups, tiles = len(rows), len(rows[0])
    sub = lax.broadcasted_iota(jnp.int32, (SUBLANES, LANES), 0)
    for j in range(groups):
        own = rows[j] + [unit[j]]
        out = list(own)
        col = {
            g: [along_lanes(rows[g][tile], lane0 + SUBLANES * j + c) for c in range(SUBLANES)] for g in range(j, groups)
        }
        pivot = {(r, c): along_sublanes(col[j][c], r) for c in range(SUBLANES) for r in range(c, SUBLANES)}
        low, done = {}, []
        for i in range(SUBLANES):
            scale = lax.rsqrt(pivot[i, i])
            for r in range(i + 1, SUBLANES):
                low[r, i] = pivot[r, i] * scale
            for c in range(i + 1, SUBLANES):
                for r in range(c, SUBLANES):
                    pivot[r, c] = pivot[r, c] - low[r, i] * low[c, i]
            solved = []
            for t in range(tiles + 1):
                x = along_sublanes(own[t], i)
                for m in range(i):
                    x = x - low[i, m] * done[m][t]
                x = x * scale
                solved.append(x)
                out[t] = jnp.where(sub == i, x, out[t])
            done.append(solved)
            for g in range(j + 1, groups):
                x = col[g][i]
                for m in range(i):
                    x = x - col[g][m] * low[i, m]
                col[g][i] = x * scale
        rows[j], unit[j] = out[:tiles], out[tiles]
        for g in range(j + 1, groups):
            for i in range(SUBLANES):
                for t in range(tiles):
                    rows[g][t] = rows[g][t] - col[g][i] * done[i][t]
                unit[g] = unit[g] - col[g][i] * done[i][tiles]


def factor_block(m_ref, r_ref, w_ref, k):
    n = m_ref.shape[0]
    tiles, groups = n // LANES, BLOCK // SUBLANES
    sub = lax.broadcasted_iota(jnp.int32, (SUBLANES, LANES), 0)
    lane = lax.broadcasted_iota(jnp.int32, (SUBLANES, LANES), 1)
    zeros = jnp.zeros((SUBLANES, LANES), jnp.float32)
    base = k * BLOCK
    tile, lane0 = base // LANES, base % LANES
    at = lambda g, t: (slice(base + SUBLANES * g, base + SUBLANES * (g + 1)), slice(LANES * t, LANES * (t + 1)))
    rows = [[m_ref[at(g, t)] for t in range(tiles)] for g in range(groups)]
    unit = [jnp.where(lane == lane0 + SUBLANES * g + sub, 1.0, 0.0).astype(jnp.float32) for g in range(groups)]
    factor_rows(rows, unit, tile, lane0)
    inside = (lane >= lane0) & (lane < lane0 + BLOCK)
    both = [[jnp.where(inside, unit[g], rows[g][t]) if t == tile else rows[g][t] for t in range(tiles)] for g in range(groups)]
    for g in range(groups):
        for t in range(tiles):
            c, r = lane + LANES * t, sub + base + SUBLANES * g
            r_ref[at(g, t)] = zeros if t < tile else rows[g][t] if t > tile else jnp.where(c >= r, rows[g][t], 0.0)
            w_ref[at(g, t)] = zeros if t > tile else rows[g][t] if t < tile else jnp.where(c <= r, both[g][t], 0.0)
    below = base + BLOCK
    if below < n:
        t0 = below // LANES
        right = jnp.concatenate([jnp.concatenate(both[g], axis=1) for g in range(groups)], axis=0)
        left = jnp.concatenate([jnp.concatenate(rows[g][t0:], axis=1) for g in range(groups)], axis=0)
        change = product(left[:, below - LANES * t0 :], right, 0, 0)
        c = lax.broadcasted_iota(jnp.int32, (n - below, n), 1)
        old = m_ref[below:, :]
        m_ref[below:, :] = jnp.where((c >= base) & (c < below), 0.0, old) - change


def factor_first_kernel(mine_ref, other_ref, m_ref, r_ref, w_ref):
    unpack(mine_ref, other_ref, m_ref)
    for k in range(m_ref.shape[0] // BLOCK // 2):
        factor_block(m_ref, r_ref, w_ref, k)


def factor_second_kernel(m_ref, r0_ref, w0_ref, r_ref, w_ref, work_ref):
    n = m_ref.shape[0]
    half = n // 2
    work_ref[...] = m_ref[...]
    r_ref[:half, :] = r0_ref[:half, :]
    w_ref[:half, :] = w0_ref[:half, :]
    for k in range(n // BLOCK // 2, n // BLOCK):
        factor_block(work_ref, r_ref, w_ref, k)


def cross_kernel(panel_ref, trailing_ref, keep_ref, send_ref):
    half = trailing_ref.shape[1] // 2
    terms = product(panel_ref[...], trailing_ref[...], 0, 0)
    even = lax.rem(lax.axis_index("rows"), 2) == 0

    @pl.when(even)
    def _():
        keep_ref[...] = terms[:, :half]
        send_ref[...] = terms[:, half:]

    @pl.when(jnp.logical_not(even))
    def _():
        keep_ref[...] = terms[:, half:]
        send_ref[...] = terms[:, :half]


def finish_kernel(w_ref, mine_ref, other_ref, panel_ref, trailing_ref, coefficients_ref, updated_ref):
    inverse = w_ref[...]
    even = lax.rem(lax.axis_index("rows"), 2) == 0
    mine, other = mine_ref[...], other_ref[...]
    terms = jnp.concatenate([jnp.where(even, mine, other), jnp.where(even, other, mine)], axis=1)
    coefficients = product(inverse, terms, 1, 0)
    coefficients_ref[...] = coefficients
    basis = product(panel_ref[...], inverse, 1, 1)
    updated_ref[...] = trailing_ref[...] - product(basis, coefficients, 1, 0)


def local(panel, trailing, *, n_rows, n_cols):
    height, width = panel.shape
    tall, wide = trailing.shape
    half = width // 2
    bits = n_rows.bit_length() - 1
    links = bits - 1
    partner = [(i, i ^ 1) for i in range(n_rows)]
    rounds = []
    for t in range(links):
        bit = [1 + t, 1 + (t + links // 2) % links]
        rounds.append([(i, i ^ (1 << bit[i % 2])) for i in range(n_rows)])

    pieces = [panel]
    for step in range(1, n_cols):
        pieces.append(lax.ppermute(panel, "cols", [(i, (i + step) % n_cols) for i in range(n_cols)]))
    packed = (half + SUBLANES, half)
    panel_block, g, g_send = call(
        functools.partial(gram_kernel, count=n_cols), [(tall, width), packed, packed], *pieces, name="gram"
    )
    g = g + lax.ppermute(g_send, "rows", partner)
    c, c_send = call(cross_kernel, [(width, wide // 2)] * 2, panel_block, trailing, name="cross")
    c = c + lax.ppermute(c_send, "rows", partner)
    for pairs in rounds:
        g = g + lax.ppermute(g, "rows", pairs)
    for pairs in rounds:
        c = c + lax.ppermute(c, "rows", pairs)
    g_other = lax.ppermute(g, "rows", partner)
    c_other = lax.ppermute(c, "rows", partner)
    m, r, w = call(factor_first_kernel, [(width, width)] * 3, g, g_other, name="factor_first")
    r, w = call(
        factor_second_kernel,
        [(width, width)] * 2,
        m,
        r,
        w,
        scratch=[pltpu.VMEM((width, width), jnp.float32)],
        name="factor_second",
    )
    coefficients, updated = call(
        finish_kernel, [(width, wide), (tall, wide)], w, c, c_other, panel_block, trailing, name="finish"
    )
    return r, coefficients, updated


def solution(mesh):
    return jax.shard_map(
        functools.partial(local, n_rows=mesh.shape["rows"], n_cols=mesh.shape["cols"]),
        mesh=mesh,
        in_specs=(P(("rows", "cols"), None), P("rows", "cols")),
        out_specs=(P(), P(None, "cols"), P("rows", "cols")),
        check_vma=False,
    )
```

time: 156 us -> 59.1 us (0.38)
  other arithmetic: 54.9 us -> 1.08 us
  waiting for transfers between devices: 57.1 us -> 21.3 us
  Pallas kernels: 0 us -> 19.1 us
  blocking collectives: 16 us -> 0 us
  between operations: 15.5 us -> 0.73 us
  starting transfers between devices: 0.04 us -> 14.4 us
  local copies, waits for them, and re-layouts: 7.43 us -> 2.23 us
  matrix products: 5.19 us -> 0 us
    psum x1 -> x0, waiting for transfers between devices: 57.1 us -> none  [local(): summed = lax.psum(stacked, 'rows')]
    another operation x9 -> x0, other arithmetic: 53.8 us -> none  [the longest x6 34.1 us: cholesky_pair(): lower = jnp.linalg.cholesky(matrix)]
    ppermute x0 -> x11, waiting for transfers between devices: none -> 21.3 us  [the longest x2 9.72 us: local(): c = c + lax.ppermute(c, 'rows', pairs)]
    pallas_call x0 -> x5, Pallas kernels: none -> 19.1 us  [call(): pl.pallas_call(body, out_shape=shapes, scratch_shapes=list(scratch), name...]
    all_gather x1 -> x0, blocking collectives: 16 us -> none  [local(): panel_block = lax.all_gather(panel, 'cols', axis=0, tiled=True)]
    ppermute x0 -> x11, starting transfers between devices: none -> 14.4 us  [the longest x3 7.95 us: local(): lax.ppermute(panel, 'cols', [(i, (i + step) % n_cols) for i in range(n_co...]
    another operation x9 -> x0, local copies, waits for them, and re-layouts: 4.05 us -> none
    dot_general x5 -> x0, matrix products: 3.89 us -> none  [the longest x3 2.29 us: product(): return jnp.dot(left, right, precision=lax.Precision.HIGHEST)]
  transfers between devices with their start and end apart: 1 -> 11, of which waited for: 1 -> 9; matrix products, arithmetic and copies ran while one was open for 0% -> 0% of each run, Pallas kernels for 0% -> 20%
where the time goes in v1:
time: 59.1 us; the launch traced here: 58.8 us
  waiting for transfers between devices  21.3 us (36%)
  Pallas kernels  19.1 us (32%)
  starting transfers between devices  14.4 us (24%)
  local copies, waits for them, and re-layouts  2.23 us (4%)
  other arithmetic  1.08 us (2%)
  between operations  0.73 us (1%)
    pallas_call x5, Pallas kernels, call(): pl.pallas_call(body, out_shape=shapes, scratch_shapes=list(scratch), name...  19.1 us
    ppermute x2, waiting for transfers between devices, local(): c = c + lax.ppermute(c, 'rows', pairs)  9.72 us
    ppermute x3, starting transfers between devices, local(): lax.ppermute(panel, 'cols', [(i, (i + step) % n_cols) for i in range(n_co...  7.95 us
    ppermute x2, waiting for transfers between devices, local(): g = g + lax.ppermute(g, 'rows', pairs)  5.61 us
    ppermute x2, starting transfers between devices, local(): c = c + lax.ppermute(c, 'rows', pairs)  3.14 us
    ppermute x2, starting transfers between devices, local(): g = g + lax.ppermute(g, 'rows', pairs)  3.14 us
    ppermute x3, waiting for transfers between devices, local(): lax.ppermute(panel, 'cols', [(i, (i + step) % n_cols) for i in range(n_co...  2.93 us
    unnamed x18, local copies, waits for them, and re-layouts  2.23 us
  transfers between devices with their start and end apart: 11, of which 9 were waited for; matrix products, arithmetic and copies ran while one was open for 0% of the time, Pallas kernels for 20%

profile of v1, /device:TPU:0, one launch (start us, length us, event | category | flops | bytes accessed | tf_op | source)
XLA Modules:
  0.0 58.8 jit_solution(1138394672285484555)
XLA Ops:
  0.6 4.1 %collective-permute-start.1 = (f32[64,256]{1,0:T(8,128)}, f32[64,256]{1,0:T(8,128)S(1)}, u32[]{:S(2)}, u32[]{:S(2)}) collective-permute-start(f32[64,256]{1,0:T(8,128)} %refs_0_.1), channel_id=1, source_target_pairs={{0,2},{1,3},{2,0},{3,1},{4,6},{5,7},{6,4},{7,5},{8,10},{9,11},{10,... | collective-permute-start | bytes 196616 | tf_op jit(solution)/shard_map/ppermute | solution.py:227
  4.8 1.6 %collective-permute-start = (f32[64,256]{1,0:T(8,128)}, f32[64,256]{1,0:T(8,128)S(1)}, u32[]{:S(2)}, u32[]{:S(2)}) collective-permute-start(f32[64,256]{1,0:T(8,128)} %refs_0_.1), channel_id=1, source_target_pairs={{0,1},{1,2},{2,3},{3,0},{4,5},{5,6},{6,7},{7,4},{8,9},{9,10},{10,1... | collective-permute-start | bytes 196616 | tf_op jit(solution)/shard_map/ppermute | solution.py:227
  6.3 2.2 %collective-permute-start.2 = (f32[64,256]{1,0:T(8,128)}, f32[64,256]{1,0:T(8,128)S(1)}, u32[]{:S(2)}, u32[]{:S(2)}) collective-permute-start(f32[64,256]{1,0:T(8,128)} %refs_0_.1), channel_id=1, source_target_pairs={{0,3},{1,0},{2,1},{3,2},{4,7},{5,4},{6,5},{7,6},{8,11},{9,8},{10,9... | collective-permute-start | bytes 196616 | tf_op jit(solution)/shard_map/ppermute | solution.py:227
  8.7 2.5 %collective-permute-done.refs_1_ = f32[64,256]{1,0:T(8,128)S(1)} collective-permute-done((f32[64,256]{1,0:T(8,128)}, f32[64,256]{1,0:T(8,128)S(1)}, u32[]{:S(2)}, u32[]{:S(2)}) %collective-permute-start) | collective-permute-done | bytes 65568 | tf_op jit(solution)/shard_map/ppermute | solution.py:227
  11.1 0.4 collective-permute-done.2.refs_3_
  11.8 0.6 %copy-done.7 = f32[64,256]{1,0:T(8,128)} copy-done((f32[64,256]{1,0:T(8,128)}, f32[64,256]{1,0:T(8,128)S(1)}, u32[]{:S(2)}) %copy-start.7) | copy-done | bytes 65560
  12.4 2.0 %gram.1 = (f32[256,256]{1,0:T(8,128)}, f32[136,128]{1,0:T(8,128)}, f32[136,128]{1,0:T(8,128)}) custom-call(f32[64,256]{1,0:T(8,128)} %refs_0_.1, f32[64,256]{1,0:T(8,128)} %copy-done.6, f32[64,256]{1,0:T(8,128)} %copy-done.5, f32[64,256]{1,0:T(8,128)} %copy-done.7), custom_call_target="tpu_custom_call" | custom-call | tf_op jit(solution)/shard_map/gram/pallas_call | solution.py:36
  14.4 2.4 %cross.1 = (f32[256,256]{1,0:T(8,128)}, f32[256,256]{1,0:T(8,128)}) custom-call(f32[256,256]{1,0:T(8,128)} %get-tuple-element.22.panel_ref, f32[256,512]{1,0:T(8,128)} %trailing_ref.3), custom_call_target="tpu_custom_call" | custom-call | tf_op jit(solution)/shard_map/cross/pallas_call | solution.py:36
  16.7 1.7 %collective-permute-done.7 = f32[256,256]{1,0:T(8,128)S(1)} collective-permute-done((f32[256,256]{1,0:T(8,128)}, f32[256,256]{1,0:T(8,128)S(1)}, u32[]{:S(2)}, u32[]{:S(2)}) %collective-permute-start.7) | collective-permute-done | bytes 262176 | tf_op jit(solution)/shard_map/ppermute | solution.py:234
  18.5 1.0 %add.21 = f32[256,256]{1,0:T(8,128)S(1)} add(f32[256,256]{1,0:T(8,128)} %get-tuple-element.23, f32[256,256]{1,0:T(8,128)S(1)} %collective-permute-done.7) | non-fusion elementwise | flops 65536 | bytes 786432 | tf_op jit(solution)/shard_map/add | solution.py:234
  19.5 1.6 %collective-permute-start.8 = (f32[256,256]{1,0:T(8,128)S(1)}, f32[256,256]{1,0:T(8,128)S(1)}, u32[]{:S(2)}, u32[]{:S(2)}) collective-permute-start(f32[256,256]{1,0:T(8,128)S(1)} %add.21), channel_id=1, source_target_pairs={{0,8},{4,20},{8,0},{12,28},{16,24},{20,4},{24,16},{28,12},{1,9},{5... | collective-permute-start | bytes 786440 | tf_op jit(solution)/shard_map/ppermute | solution.py:238
  21.0 4.9 %collective-permute-done.8 = f32[256,256]{1,0:T(8,128)S(1)} collective-permute-done((f32[256,256]{1,0:T(8,128)S(1)}, f32[256,256]{1,0:T(8,128)S(1)}, u32[]{:S(2)}, u32[]{:S(2)}) %collective-permute-start.8) | collective-permute-done | bytes 262176 | tf_op jit(solution)/shard_map/ppermute | solution.py:238
  26.0 1.6 %collective-permute-start.9 = (f32[256,256]{1,0:T(8,128)S(1)}, f32[256,256]{1,0:T(8,128)S(1)}, u32[]{:S(2)}, u32[]{:S(2)}) collective-permute-start(f32[256,256]{1,0:T(8,128)S(1)} %add.22), channel_id=1, source_target_pairs={{0,16},{4,12},{8,24},{12,4},{16,0},{20,28},{24,8},{28,20},{1,17},{... | collective-permute-start | bytes 786440 | tf_op jit(solution)/shard_map/ppermute | solution.py:238
  27.6 4.8 %collective-permute-done.9 = f32[256,256]{1,0:T(8,128)S(1)} collective-permute-done((f32[256,256]{1,0:T(8,128)S(1)}, f32[256,256]{1,0:T(8,128)S(1)}, u32[]{:S(2)}, u32[]{:S(2)}) %collective-permute-start.9) | collective-permute-done | bytes 262176 | tf_op jit(solution)/shard_map/ppermute | solution.py:238
  32.6 1.6 %collective-permute-start.4 = (f32[136,128]{1,0:T(8,128)S(1)}, f32[136,128]{1,0:T(8,128)S(1)}, u32[]{:S(2)}, u32[]{:S(2)}) collective-permute-start(f32[136,128]{1,0:T(8,128)S(1)} %add.18), channel_id=1, source_target_pairs={{0,8},{4,20},{8,0},{12,28},{16,24},{20,4},{24,16},{28,12},{1,9},{5... | collective-permute-start | bytes 208904 | tf_op jit(solution)/shard_map/ppermute | solution.py:236
  34.1 2.8 %collective-permute-done.4 = f32[136,128]{1,0:T(8,128)S(1)} collective-permute-done((f32[136,128]{1,0:T(8,128)S(1)}, f32[136,128]{1,0:T(8,128)S(1)}, u32[]{:S(2)}, u32[]{:S(2)}) %collective-permute-start.4) | collective-permute-done | bytes 69664 | tf_op jit(solution)/shard_map/ppermute | solution.py:236
  37.0 1.6 %collective-permute-start.5 = (f32[136,128]{1,0:T(8,128)S(1)}, f32[136,128]{1,0:T(8,128)S(1)}, u32[]{:S(2)}, u32[]{:S(2)}) collective-permute-start(f32[136,128]{1,0:T(8,128)S(1)} %add.19), channel_id=1, source_target_pairs={{0,16},{4,12},{8,24},{12,4},{16,0},{20,28},{24,8},{28,20},{1,17},{... | collective-permute-start | bytes 208904 | tf_op jit(solution)/shard_map/ppermute | solution.py:236
  38.5 2.8 %collective-permute-done.5 = f32[136,128]{1,0:T(8,128)S(1)} collective-permute-done((f32[136,128]{1,0:T(8,128)S(1)}, f32[136,128]{1,0:T(8,128)S(1)}, u32[]{:S(2)}, u32[]{:S(2)}) %collective-permute-start.5) | collective-permute-done | bytes 69664 | tf_op jit(solution)/shard_map/ppermute | solution.py:236
  41.4 1.2 %collective-permute-done.6.other_ref = f32[136,128]{1,0:T(8,128)S(1)} collective-permute-done((f32[136,128]{1,0:T(8,128)S(1)}, f32[136,128]{1,0:T(8,128)S(1)}, u32[]{:S(2)}, u32[]{:S(2)}) %collective-permute-start.6) | collective-permute-done | bytes 69664 | tf_op jit(solution)/shard_map/ppermute | solution.py:239
  42.7 0.6 %copy-done.4 = f32[136,128]{1,0:T(8,128)} copy-done((f32[136,128]{1,0:T(8,128)}, f32[136,128]{1,0:T(8,128)S(1)}, u32[]{:S(2)}) %copy-start.4) | copy-done | bytes 69656
  43.3 5.9 %factor_first.1 = (f32[256,256]{1,0:T(8,128)}, f32[256,256]{1,0:T(8,128)}, f32[256,256]{1,0:T(8,128)}) custom-call(f32[136,128]{1,0:T(8,128)} %copy-done.1, f32[136,128]{1,0:T(8,128)} %copy-done.4), custom_call_target="tpu_custom_call" | custom-call | tf_op jit(solution)/shard_map/factor_first/pallas_call | solution.py:36
  49.3 5.9 %factor_second.1 = (f32[256,256]{1,0:T(8,128)}, f32[256,256]{1,0:T(8,128)}) custom-call(f32[256,256]{1,0:T(8,128)} %get-tuple-element.17.m_ref, f32[256,256]{1,0:T(8,128)} %get-tuple-element.18.r0_ref, f32[256,256]{1,0:T(8,128)} %get-tuple-element.19.w0_ref), custom_call_target="tpu_custom_call" | custom-call | tf_op jit(solution)/shard_map/factor_second/pallas_call | solution.py:36
  55.2 0.7 %copy-done.2 = f32[256,256]{1,0:T(8,128)} copy-done((f32[256,256]{1,0:T(8,128)}, f32[256,256]{1,0:T(8,128)S(1)}, u32[]{:S(2)}) %copy-start.2) | copy-done | bytes 262168
  55.9 3.0 %finish.1 = (f32[256,512]{1,0:T(8,128)}, f32[256,512]{1,0:T(8,128)}) custom-call(f32[256,256]{1,0:T(8,128)} %get-tuple-element.21.w_ref, f32[256,256]{1,0:T(8,128)} %copy-done, f32[256,256]{1,0:T(8,128)} %copy-done.2, f32[256,256]{1,0:T(8,128)} %get-tuple-element.22.panel_ref, f32[256,512]{1,0:T(8,128)} %trailing_ref.3), custom_call_target="tpu_custom_call" | custom-call | tf_op jit(solution)/shard_map/finish/pallas_call | solution.py:36
  (27 shorter events, 0.6 us)
Async XLA Ops:
  0.6 8.1 %collective-permute-start.1 = (f32[64,256]{1,0:T(8,128)}, f32[64,256]{1,0:T(8,128)S(1)}, u32[]{:S(2)}, u32[]{:S(2)}) collective-permute-start(f32[64,256]{1,0:T(8,128)} %refs_0_.1), channel_id=1, source_target_pairs={{0,2},{1,3},{2,0},{3,1},{4,6},{5,7},{6,4},{7,5},{8,10},{9,11},{10,... | collective-permute-start | bytes 196616 | tf_op jit(solution)/shard_map/ppermute | solution.py:227
  4.8 6.4 %collective-permute-start = (f32[64,256]{1,0:T(8,128)}, f32[64,256]{1,0:T(8,128)S(1)}, u32[]{:S(2)}, u32[]{:S(2)}) collective-permute-start(f32[64,256]{1,0:T(8,128)} %refs_0_.1), channel_id=1, source_target_pairs={{0,1},{1,2},{2,3},{3,0},{4,5},{5,6},{6,7},{7,4},{8,9},{9,10},{10,1... | collective-permute-start | bytes 196616 | tf_op jit(solution)/shard_map/ppermute | solution.py:227
  6.3 5.2 %collective-permute-start.2 = (f32[64,256]{1,0:T(8,128)}, f32[64,256]{1,0:T(8,128)S(1)}, u32[]{:S(2)}, u32[]{:S(2)}) collective-permute-start(f32[64,256]{1,0:T(8,128)} %refs_0_.1), channel_id=1, source_target_pairs={{0,3},{1,0},{2,1},{3,2},{4,7},{5,4},{6,5},{7,6},{8,11},{9,8},{10,9... | collective-permute-start | bytes 196616 | tf_op jit(solution)/shard_map/ppermute | solution.py:227
  8.7 2.8 %copy-start.5 = (f32[64,256]{1,0:T(8,128)}, f32[64,256]{1,0:T(8,128)S(1)}, u32[]{:S(2)}) copy-start(f32[64,256]{1,0:T(8,128)S(1)} %collective-permute-done.1.refs_2_) | copy-start | bytes 196612
  11.1 0.6 %copy-start.6 = (f32[64,256]{1,0:T(8,128)}, f32[64,256]{1,0:T(8,128)S(1)}, u32[]{:S(2)}) copy-start(f32[64,256]{1,0:T(8,128)S(1)} %collective-permute-done.refs_1_) | copy-start | bytes 196612
  11.8 0.6 %copy-start.7 = (f32[64,256]{1,0:T(8,128)}, f32[64,256]{1,0:T(8,128)S(1)}, u32[]{:S(2)}) copy-start(f32[64,256]{1,0:T(8,128)S(1)} %collective-permute-done.2.refs_3_) | copy-start | bytes 196612
  16.7 1.7 %collective-permute-start.7 = (f32[256,256]{1,0:T(8,128)}, f32[256,256]{1,0:T(8,128)S(1)}, u32[]{:S(2)}, u32[]{:S(2)}) collective-permute-start(f32[256,256]{1,0:T(8,128)} %get-tuple-element.24), channel_id=1, source_target_pairs={{0,4},{4,0},{8,12},{12,8},{16,20},{20,16},{24,28},{28,24},{1,5},{5... | collective-permute-start | bytes 786440 | tf_op jit(solution)/shard_map/ppermute | solution.py:234
  19.5 8.1 %copy-start.8 = (f32[136,128]{1,0:T(8,128)S(1)}, f32[136,128]{1,0:T(8,128)}, u32[]{:S(2)}) copy-start(f32[136,128]{1,0:T(8,128)} %get-tuple-element.16) | copy-start | bytes 208900
  19.5 6.4 %collective-permute-start.8 = (f32[256,256]{1,0:T(8,128)S(1)}, f32[256,256]{1,0:T(8,128)S(1)}, u32[]{:S(2)}, u32[]{:S(2)}) collective-permute-start(f32[256,256]{1,0:T(8,128)S(1)} %add.21), channel_id=1, source_target_pairs={{0,8},{4,20},{8,0},{12,28},{16,24},{20,4},{24,16},{28,12},{1,9},{5... | collective-permute-start | bytes 786440 | tf_op jit(solution)/shard_map/ppermute | solution.py:238
  26.0 6.4 %collective-permute-start.9 = (f32[256,256]{1,0:T(8,128)S(1)}, f32[256,256]{1,0:T(8,128)S(1)}, u32[]{:S(2)}, u32[]{:S(2)}) collective-permute-start(f32[256,256]{1,0:T(8,128)S(1)} %add.22), channel_id=1, source_target_pairs={{0,16},{4,12},{8,24},{12,4},{16,0},{20,28},{24,8},{28,20},{1,17},{... | collective-permute-start | bytes 786440 | tf_op jit(solution)/shard_map/ppermute | solution.py:238
  27.6 5.0 %copy-start.3 = (f32[136,128]{1,0:T(8,128)S(1)}, f32[136,128]{1,0:T(8,128)}, u32[]{:S(2)}) copy-start(f32[136,128]{1,0:T(8,128)} %get-tuple-element.15) | copy-start | bytes 208900
  27.6 5.0 %collective-permute-start.3 = (f32[136,128]{1,0:T(8,128)S(1)}, f32[136,128]{1,0:T(8,128)S(1)}, u32[]{:S(2)}, u32[]{:S(2)}) collective-permute-start(f32[136,128]{1,0:T(8,128)S(1)} %copy-done.8), channel_id=1, source_target_pairs={{0,4},{4,0},{8,12},{12,8},{16,20},{20,16},{24,28},{28,24},{1,5},{5... | collective-permute-start | bytes 208904 | tf_op jit(solution)/shard_map/ppermute | solution.py:232
  32.4 8.9 %copy-start = (f32[256,256]{1,0:T(8,128)}, f32[256,256]{1,0:T(8,128)S(1)}, u32[]{:S(2)}) copy-start(f32[256,256]{1,0:T(8,128)S(1)} %add.23.mine_ref) | copy-start | bytes 786436
  32.4 22.7 %collective-permute-start.10 = (f32[256,256]{1,0:T(8,128)S(1)}, f32[256,256]{1,0:T(8,128)S(1)}, u32[]{:S(2)}, u32[]{:S(2)}) collective-permute-start(f32[256,256]{1,0:T(8,128)S(1)} %add.23.mine_ref), channel_id=1, source_target_pairs={{0,4},{4,0},{8,12},{12,8},{16,20},{20,16},{24,28},{28,24},{1,5},{5... | collective-permute-start | bytes 786440 | tf_op jit(solution)/shard_map/ppermute | solution.py:240
  32.6 4.4 %collective-permute-start.4 = (f32[136,128]{1,0:T(8,128)S(1)}, f32[136,128]{1,0:T(8,128)S(1)}, u32[]{:S(2)}, u32[]{:S(2)}) collective-permute-start(f32[136,128]{1,0:T(8,128)S(1)} %add.18), channel_id=1, source_target_pairs={{0,8},{4,20},{8,0},{12,28},{16,24},{20,4},{24,16},{28,12},{1,9},{5... | collective-permute-start | bytes 208904 | tf_op jit(solution)/shard_map/ppermute | solution.py:236
  37.0 4.4 %collective-permute-start.5 = (f32[136,128]{1,0:T(8,128)S(1)}, f32[136,128]{1,0:T(8,128)S(1)}, u32[]{:S(2)}, u32[]{:S(2)}) collective-permute-start(f32[136,128]{1,0:T(8,128)S(1)} %add.19), channel_id=1, source_target_pairs={{0,16},{4,12},{8,24},{12,4},{16,0},{20,28},{24,8},{28,20},{1,17},{... | collective-permute-start | bytes 208904 | tf_op jit(solution)/shard_map/ppermute | solution.py:236
  41.3 1.3 %copy-start.1 = (f32[136,128]{1,0:T(8,128)}, f32[136,128]{1,0:T(8,128)S(1)}, u32[]{:S(2)}) copy-start(f32[136,128]{1,0:T(8,128)S(1)} %add.20.mine_ref) | copy-start | bytes 208900
  41.4 1.3 %collective-permute-start.6 = (f32[136,128]{1,0:T(8,128)S(1)}, f32[136,128]{1,0:T(8,128)S(1)}, u32[]{:S(2)}, u32[]{:S(2)}) collective-permute-start(f32[136,128]{1,0:T(8,128)S(1)} %add.20.mine_ref), channel_id=1, source_target_pairs={{0,4},{4,0},{8,12},{12,8},{16,20},{20,16},{24,28},{28,24},{1,5},{5... | collective-permute-start | bytes 208904 | tf_op jit(solution)/shard_map/ppermute | solution.py:239
  42.7 0.6 %copy-start.4 = (f32[136,128]{1,0:T(8,128)}, f32[136,128]{1,0:T(8,128)S(1)}, u32[]{:S(2)}) copy-start(f32[136,128]{1,0:T(8,128)S(1)} %collective-permute-done.6.other_ref) | copy-start | bytes 208900
  55.2 0.7 %copy-start.2 = (f32[256,256]{1,0:T(8,128)}, f32[256,256]{1,0:T(8,128)S(1)}, u32[]{:S(2)}) copy-start(f32[256,256]{1,0:T(8,128)S(1)} %collective-permute-done.10.other_ref) | copy-start | bytes 786436

commit v2 on v1

--- a/solution.py
+++ b/solution.py
@@ -7,7 +7,8 @@
 from jax.experimental.pallas import tpu as pltpu
 from jax.sharding import PartitionSpec as P
 
-LANES, SUBLANES, BLOCK = 128, 8, 32
+
+LANES, SUBLANES, BLOCK, PARTS = 128, 8, 32, 4
 
 
 def split(x):
@@ -26,14 +27,23 @@
     )
 
 
-def call(body, outs, *args, scratch=(), name=None, in_specs=None, out_specs=None):
-    shapes = [jax.ShapeDtypeStruct(s, jnp.float32) for s in outs]
-    extra = {}
-    if in_specs is not None:
-        extra["in_specs"] = in_specs
-    if out_specs is not None:
-        extra["out_specs"] = out_specs
-    return pl.pallas_call(body, out_shape=shapes, scratch_shapes=list(scratch), name=name, **extra)(*args)
+def call(body, outs, *args, aliases=None, in_vmem=True, **extra):
+    block = pl.BlockSpec(memory_space=pltpu.VMEM)
+    shapes = [(pltpu.VMEM if in_vmem else jax.ShapeDtypeStruct)(s, jnp.float32) for s in outs]
+    args = [pltpu.with_memory_space_constraint(x, pltpu.VMEM) for x in args]
+    extra = {"in_specs": [block] * len(args), "out_specs": [block] * len(outs)} | extra
+    return pl.pallas_call(body, out_shape=shapes, input_output_aliases=aliases or {}, **extra)(*args)
+
+
+def stage_kernel(panel_hbm, trailing_hbm, panel_ref, trailing_ref, sems):
+    copies = [
+        pltpu.make_async_copy(panel_hbm, panel_ref, sems.at[0]),
+        pltpu.make_async_copy(trailing_hbm, trailing_ref, sems.at[1]),
+    ]
+    for copy in copies:
+        copy.start()
+    for copy in copies:
+        copy.wait()
 
 
 def gram_kernel(*refs, count):
@@ -167,20 +177,15 @@
         m_ref[below:, :] = jnp.where((c >= base) & (c < below), 0.0, old) - change
 
 
-def factor_first_kernel(mine_ref, other_ref, m_ref, r_ref, w_ref):
+def factor_first_kernel(mine_ref, other_ref, m_ref, r_ref, w_ref, *, stop):
     unpack(mine_ref, other_ref, m_ref)
-    for k in range(m_ref.shape[0] // BLOCK // 2):
+    for k in range(stop):
         factor_block(m_ref, r_ref, w_ref, k)
 
 
-def factor_second_kernel(m_ref, r0_ref, w0_ref, r_ref, w_ref, work_ref):
-    n = m_ref.shape[0]
-    half = n // 2
-    work_ref[...] = m_ref[...]
-    r_ref[:half, :] = r0_ref[:half, :]
-    w_ref[:half, :] = w0_ref[:half, :]
-    for k in range(n // BLOCK // 2, n // BLOCK):
-        factor_block(work_ref, r_ref, w_ref, k)
+def factor_more_kernel(m0_ref, r0_ref, w0_ref, m_ref, r_ref, w_ref, *, start, stop):
+    for k in range(start, stop):
+        factor_block(m_ref, r_ref, w_ref, k)
 
 
 def cross_kernel(panel_ref, trailing_ref, keep_ref, send_ref):
@@ -199,19 +204,28 @@
         send_ref[...] = terms[:, :half]
 
 
-def finish_kernel(w_ref, mine_ref, other_ref, panel_ref, trailing_ref, coefficients_ref, updated_ref):
+def finish_kernel(w_ref, mine_ref, other_ref, panel_ref, trailing_ref, coefficients_ref, updated_ref, c_ref, u_ref, sems):
     inverse = w_ref[...]
     even = lax.rem(lax.axis_index("rows"), 2) == 0
     mine, other = mine_ref[...], other_ref[...]
     terms = jnp.concatenate([jnp.where(even, mine, other), jnp.where(even, other, mine)], axis=1)
     coefficients = product(inverse, terms, 1, 0)
-    coefficients_ref[...] = coefficients
+    c_ref[...] = coefficients
+    copies = [pltpu.make_async_copy(c_ref, coefficients_ref, sems.at[0])]
+    copies[0].start()
     basis = product(panel_ref[...], inverse, 1, 1)
-    updated_ref[...] = trailing_ref[...] - product(basis, coefficients, 1, 0)
+    tall = u_ref.shape[0] // PARTS
+    for part in range(PARTS):
+        at = slice(part * tall, (part + 1) * tall)
+        u_ref[at, :] = trailing_ref[at, :] - product(basis[at, :], coefficients, 1, 0)
+        copies.append(pltpu.make_async_copy(u_ref.at[at, :], updated_ref.at[at, :], sems.at[1 + part]))
+        copies[-1].start()
+    for copy in copies:
+        copy.wait()
 
 
 def local(panel, trailing, *, n_rows, n_cols):
-    height, width = panel.shape
+    _, width = panel.shape
     tall, wide = trailing.shape
     half = width // 2
     bits = n_rows.bit_length() - 1
@@ -222,41 +236,75 @@
         bit = [1 + t, 1 + (t + links // 2) % links]
         rounds.append([(i, i ^ (1 << bit[i % 2])) for i in range(n_rows)])
 
-    pieces = [panel]
+    def sent(x, pairs, axis="rows"):
+        return lax.ppermute(x, axis, pairs)
+
+    def summed(x, pairs):
+        y = sent(x, pairs)
+        return x + y
+
+    panel_here, trailing = pl.pallas_call(
+        stage_kernel,
+        out_shape=[pltpu.VMEM(x.shape, x.dtype) for x in (panel, trailing)],
+        in_specs=[pl.BlockSpec(memory_space=pl.ANY)] * 2,
+        out_specs=[pl.BlockSpec(memory_space=pltpu.VMEM)] * 2,
+        scratch_shapes=[pltpu.SemaphoreType.DMA((2,))],
+        name="stage",
+    )(panel, trailing)
+    pieces = [panel_here]
     for step in range(1, n_cols):
-        pieces.append(lax.ppermute(panel, "cols", [(i, (i + step) % n_cols) for i in range(n_cols)]))
-    packed = (half + SUBLANES, half)
+        pieces.append(sent(panel, [(i, (i + step) % n_cols) for i in range(n_cols)], "cols"))
+    packed, square = (half + SUBLANES, half), (width, width)
     panel_block, g, g_send = call(
-        functools.partial(gram_kernel, count=n_cols), [(tall, width), packed, packed], *pieces, name="gram"
+        functools.partial(gram_kernel, count=n_cols), [(tall, width), packed, packed], *pieces
     )
-    g = g + lax.ppermute(g_send, "rows", partner)
-    c, c_send = call(cross_kernel, [(width, wide // 2)] * 2, panel_block, trailing, name="cross")
-    c = c + lax.ppermute(c_send, "rows", partner)
+    g = g + sent(g_send, partner)
+    c, c_send = call(cross_kernel, [(width, wide // 2)] * 2, panel_block, trailing)
+    c_got = sent(c_send, partner)
+    c = c + c_got
     for pairs in rounds:
-        g = g + lax.ppermute(g, "rows", pairs)
-    for pairs in rounds:
-        c = c + lax.ppermute(c, "rows", pairs)
-    g_other = lax.ppermute(g, "rows", partner)
-    c_other = lax.ppermute(c, "rows", partner)
-    m, r, w = call(factor_first_kernel, [(width, width)] * 3, g, g_other, name="factor_first")
-    r, w = call(
-        factor_second_kernel,
-        [(width, width)] * 2,
-        m,
-        r,
+        g = summed(g, pairs)
+    g_other = sent(g, partner)
+    for pairs in rounds[:-1]:
+        c = summed(c, pairs)
+    blocks = width // BLOCK
+    cuts = [blocks * 3 // 8, blocks * 7 // 8, blocks]
+    state = call(functools.partial(factor_first_kernel, stop=cuts[0]), [square] * 3, g, g_other)
+    c = summed(c, rounds[-1])
+    for i in (1, 2):
+        state = call(
+            functools.partial(factor_more_kernel, start=cuts[i - 1], stop=cuts[i]),
+            [square] * 3,
+            *state,
+            aliases={0: 0, 1: 1, 2: 2},
+        )
+        if i == 1:
+            c_other = sent(c, partner)
+    _, r, w = state
+    hbm = pl.BlockSpec(memory_space=pl.ANY)
+    coefficients, updated = call(
+        finish_kernel,
+        [(width, wide), (tall, wide)],
         w,
-        scratch=[pltpu.VMEM((width, width), jnp.float32)],
-        name="factor_second",
-    )
-    coefficients, updated = call(
-        finish_kernel, [(width, wide), (tall, wide)], w, c, c_other, panel_block, trailing, name="finish"
+        c,
+        c_other,
+        panel_block,
+        trailing,
+        in_vmem=False,
+        out_specs=[hbm, hbm],
+        scratch_shapes=[
+            pltpu.VMEM((width, wide), jnp.float32),
+            pltpu.VMEM((tall, wide), jnp.float32),
+            pltpu.SemaphoreType.DMA((1 + PARTS,)),
+        ],
     )
     return r, coefficients, updated
 
 
 def solution(mesh):
+    n_rows = mesh.shape["rows"]
     return jax.shard_map(
-        functools.partial(local, n_rows=mesh.shape["rows"], n_cols=mesh.shape["cols"]),
+        functools.partial(local, n_rows=n_rows, n_cols=mesh.shape["cols"]),
         mesh=mesh,
         in_specs=(P(("rows", "cols"), None), P("rows", "cols")),
         out_specs=(P(), P(None, "cols"), P("rows", "cols")),

time: 59.1 us -> 48.9 us (0.83)
  Pallas kernels: 19.1 us -> 12 us
  starting transfers between devices: 14.4 us -> 12.7 us
  local copies, waits for them, and re-layouts: 2.23 us -> 0.71 us
  waiting for transfers between devices: 21.3 us -> 22.5 us
  other arithmetic: 1.08 us -> 0.14 us
    pallas_call x5 -> x7, Pallas kernels: 19.1 us -> 12 us  [the longest x6 10.9 us: call(): pl.pallas_call(body, out_shape=shapes, input_output_aliases=aliases or {}...]
    ppermute x11, starting transfers between devices: 14.4 us -> 12.7 us  [sent(): return lax.ppermute(x, axis, pairs)]
    unnamed x18 -> x1, local copies, waits for them, and re-layouts: 2.23 us -> 0.71 us
    ppermute x11, waiting for transfers between devices: 21.3 us -> 22.5 us  [sent(): return lax.ppermute(x, axis, pairs)]
    add x6, other arithmetic: 1.08 us -> 0.14 us  [the longest x4 0.09 us: summed(): return x + y]
  transfers between devices with their start and end apart: 11 -> 11, of which waited for: 9 -> 9; matrix products, arithmetic and copies ran while one was open for 0% -> 2% of each run, Pallas kernels for 20% -> 19%
where the time goes in v2:
time: 48.9 us; the launch traced here: 48.7 us
  waiting for transfers between devices  22.5 us (46%)
  starting transfers between devices  12.7 us (26%)
  Pallas kernels  12 us (25%)
  between operations  0.73 us (1%)
  local copies, waits for them, and re-layouts  0.71 us (1%)
    ppermute x11, waiting for transfers between devices, sent(): return lax.ppermute(x, axis, pairs)  22.5 us
    ppermute x11, starting transfers between devices, sent(): return lax.ppermute(x, axis, pairs)  12.7 us
    pallas_call x6, Pallas kernels, call(): pl.pallas_call(body, out_shape=shapes, input_output_aliases=aliases or {}...  10.9 us
    pallas_call x1, Pallas kernels, local(): pl.pallas_call(stage_kernel, out_shape=[pltpu.VMEM(x.shape, x.dtype) for...  1.1 us
  transfers between devices with their start and end apart: 11, of which 9 were waited for; matrix products, arithmetic and copies ran while one was open for 2% of the time, Pallas kernels for 19%

profile of v2, /device:TPU:0, one launch (start us, length us, event | category | flops | bytes accessed | tf_op | source)
XLA Modules:
  0.0 48.7 jit_solution(2335751803138803655)
XLA Ops:
  0.6 3.1 %collective-permute-start = (f32[64,256]{1,0:T(8,128)}, f32[64,256]{1,0:T(8,128)S(1)}, u32[]{:S(2)}, u32[]{:S(2)}) collective-permute-start(f32[64,256]{1,0:T(8,128)} %panel_hbm.1), channel_id=1, source_target_pairs={{0,1},{1,2},{2,3},{3,0},{4,5},{5,6},{6,7},{7,4},{8,9},{9,10},{10,1... | collective-permute-start | bytes 196616 | tf_op jit(solution)/shard_map/ppermute | solution.py:240
  3.7 2.1 %collective-permute-start.2 = (f32[64,256]{1,0:T(8,128)}, f32[64,256]{1,0:T(8,128)S(1)}, u32[]{:S(2)}, u32[]{:S(2)}) collective-permute-start(f32[64,256]{1,0:T(8,128)} %panel_hbm.1), channel_id=1, source_target_pairs={{0,3},{1,0},{2,1},{3,2},{4,7},{5,4},{6,5},{7,6},{8,11},{9,8},{10,9... | collective-permute-start | bytes 196616 | tf_op jit(solution)/shard_map/ppermute | solution.py:240
  5.8 0.9 %collective-permute-start.1 = (f32[64,256]{1,0:T(8,128)}, f32[64,256]{1,0:T(8,128)S(1)}, u32[]{:S(2)}, u32[]{:S(2)}) collective-permute-start(f32[64,256]{1,0:T(8,128)} %panel_hbm.1), channel_id=1, source_target_pairs={{0,2},{1,3},{2,0},{3,1},{4,6},{5,7},{6,4},{7,5},{8,10},{9,11},{10,... | collective-permute-start | bytes 196616 | tf_op jit(solution)/shard_map/ppermute | solution.py:240
  6.8 1.1 %stage.1 = (f32[64,256]{1,0:T(8,128)S(1)}, f32[256,512]{1,0:T(8,128)S(1)}) custom-call(f32[64,256]{1,0:T(8,128)} %panel_hbm.1, f32[256,512]{1,0:T(8,128)} %trailing_hbm.1), custom_call_target="tpu_custom_call" | custom-call | tf_op jit(solution)/shard_map/stage/pallas_call | solution.py:246
  7.9 0.4 collective-permute-done.refs_1_
  8.3 0.6 %collective-permute-done.2.refs_3_ = f32[64,256]{1,0:T(8,128)S(1)} collective-permute-done((f32[64,256]{1,0:T(8,128)}, f32[64,256]{1,0:T(8,128)S(1)}, u32[]{:S(2)}, u32[]{:S(2)}) %collective-permute-start.2) | collective-permute-done | bytes 65568 | tf_op jit(solution)/shard_map/ppermute | solution.py:240
  8.9 3.4 %collective-permute-done.1.refs_2_ = f32[64,256]{1,0:T(8,128)S(1)} collective-permute-done((f32[64,256]{1,0:T(8,128)}, f32[64,256]{1,0:T(8,128)S(1)}, u32[]{:S(2)}, u32[]{:S(2)}) %collective-permute-start.1) | collective-permute-done | bytes 65568 | tf_op jit(solution)/shard_map/ppermute | solution.py:240
  12.3 0.3 shard_map.49
  12.6 0.4 shard_map.53
  13.1 1.5 %collective-permute-done.7 = f32[256,256]{1,0:T(8,128)S(1)} collective-permute-done((f32[256,256]{1,0:T(8,128)S(1)}, f32[256,256]{1,0:T(8,128)S(1)}, u32[]{:S(2)}, u32[]{:S(2)}) %collective-permute-start.7) | collective-permute-done | bytes 262176 | tf_op jit(solution)/shard_map/ppermute | solution.py:240
  14.7 1.6 %collective-permute-start.8 = (f32[256,256]{1,0:T(8,128)S(1)}, f32[256,256]{1,0:T(8,128)S(1)}, u32[]{:S(2)}, u32[]{:S(2)}) collective-permute-start(f32[256,256]{1,0:T(8,128)S(1)} %add.21), channel_id=1, source_target_pairs={{0,8},{4,20},{8,0},{12,28},{16,24},{20,4},{24,16},{28,12},{1,9},{5... | collective-permute-start | bytes 786440 | tf_op jit(solution)/shard_map/ppermute | solution.py:240
  16.3 4.9 %collective-permute-done.8 = f32[256,256]{1,0:T(8,128)S(1)} collective-permute-done((f32[256,256]{1,0:T(8,128)S(1)}, f32[256,256]{1,0:T(8,128)S(1)}, u32[]{:S(2)}, u32[]{:S(2)}) %collective-permute-start.8) | collective-permute-done | bytes 262176 | tf_op jit(solution)/shard_map/ppermute | solution.py:240
  21.2 1.6 %collective-permute-start.9 = (f32[256,256]{1,0:T(8,128)S(1)}, f32[256,256]{1,0:T(8,128)S(1)}, u32[]{:S(2)}, u32[]{:S(2)}) collective-permute-start(f32[256,256]{1,0:T(8,128)S(1)} %add.22), channel_id=1, source_target_pairs={{0,16},{4,12},{8,24},{12,4},{16,0},{20,28},{24,8},{28,20},{1,17},{... | collective-permute-start | bytes 786440 | tf_op jit(solution)/shard_map/ppermute | solution.py:240
  22.8 4.8 %collective-permute-done.9 = f32[256,256]{1,0:T(8,128)S(1)} collective-permute-done((f32[256,256]{1,0:T(8,128)S(1)}, f32[256,256]{1,0:T(8,128)S(1)}, u32[]{:S(2)}, u32[]{:S(2)}) %collective-permute-start.9) | collective-permute-done | bytes 262176 | tf_op jit(solution)/shard_map/ppermute | solution.py:240
  27.8 1.6 %collective-permute-start.4 = (f32[136,128]{1,0:T(8,128)S(1)}, f32[136,128]{1,0:T(8,128)S(1)}, u32[]{:S(2)}, u32[]{:S(2)}) collective-permute-start(f32[136,128]{1,0:T(8,128)S(1)} %add.18), channel_id=1, source_target_pairs={{0,8},{4,20},{8,0},{12,28},{16,24},{20,4},{24,16},{28,12},{1,9},{5... | collective-permute-start | bytes 208904 | tf_op jit(solution)/shard_map/ppermute | solution.py:240
  29.3 2.8 %collective-permute-done.4 = f32[136,128]{1,0:T(8,128)S(1)} collective-permute-done((f32[136,128]{1,0:T(8,128)S(1)}, f32[136,128]{1,0:T(8,128)S(1)}, u32[]{:S(2)}, u32[]{:S(2)}) %collective-permute-start.4) | collective-permute-done | bytes 69664 | tf_op jit(solution)/shard_map/ppermute | solution.py:240
  32.1 1.6 %collective-permute-start.5 = (f32[136,128]{1,0:T(8,128)S(1)}, f32[136,128]{1,0:T(8,128)S(1)}, u32[]{:S(2)}, u32[]{:S(2)}) collective-permute-start(f32[136,128]{1,0:T(8,128)S(1)} %add.19), channel_id=1, source_target_pairs={{0,16},{4,12},{8,24},{12,4},{16,0},{20,28},{24,8},{28,20},{1,17},{... | collective-permute-start | bytes 208904 | tf_op jit(solution)/shard_map/ppermute | solution.py:240
  33.7 2.8 %collective-permute-done.5 = f32[136,128]{1,0:T(8,128)S(1)} collective-permute-done((f32[136,128]{1,0:T(8,128)S(1)}, f32[136,128]{1,0:T(8,128)S(1)}, u32[]{:S(2)}, u32[]{:S(2)}) %collective-permute-start.5) | collective-permute-done | bytes 69664 | tf_op jit(solution)/shard_map/ppermute | solution.py:240
  36.6 1.2 %collective-permute-done.6.other_ref = f32[136,128]{1,0:T(8,128)S(1)} collective-permute-done((f32[136,128]{1,0:T(8,128)S(1)}, f32[136,128]{1,0:T(8,128)S(1)}, u32[]{:S(2)}, u32[]{:S(2)}) %collective-permute-start.6) | collective-permute-done | bytes 69664 | tf_op jit(solution)/shard_map/ppermute | solution.py:240
  37.9 3.3 %shard_map.50 = (f32[256,256]{1,0:T(8,128)S(1)}, f32[256,256]{1,0:T(8,128)S(1)}, f32[256,256]{1,0:T(8,128)S(1)}) custom-call(f32[136,128]{1,0:T(8,128)S(1)} %add.20.mine_ref, f32[136,128]{1,0:T(8,128)S(1)} %collective-permute-done.6.other_ref), custom_call_target="tpu_custom_call" | custom-call | tf_op jit(solution)/shard_map/pallas_call | solution.py:35
  41.2 4.2 %shard_map.51 = (f32[256,256]{1,0:T(8,128)S(1)}, f32[256,256]{1,0:T(8,128)S(1)}, f32[256,256]{1,0:T(8,128)S(1)}) custom-call(f32[256,256]{1,0:T(8,128)S(1)} %get-tuple-element.23.m0_ref, f32[256,256]{1,0:T(8,128)S(1)} %get-tuple-element.24.r0_ref, f32[256,256]{1,0:T(8,128)S(1)} %get-tuple-element.25.w0_ref), custom_call_target="tpu_custom_call", output_to_operand_aliasing={{0}: (0, {}), {1}: (1, {}), {2}: (2, {})} | custom-call | tf_op jit(solution)/shard_map/pallas_call | solution.py:35
  45.3 0.8 %shard_map.52 = (f32[256,256]{1,0:T(8,128)S(1)}, f32[256,256]{1,0:T(8,128)S(1)}, f32[256,256]{1,0:T(8,128)S(1)}) custom-call(f32[256,256]{1,0:T(8,128)S(1)} %get-tuple-element.26.m0_ref, f32[256,256]{1,0:T(8,128)S(1)} %get-tuple-element.27.r0_ref, f32[256,256]{1,0:T(8,128)S(1)} %get-tuple-element.28.w0_ref), custom_call_target="tpu_custom_call", output_to_operand_aliasing={{0}: (0, {}), {1}: (1, {}), {2}: (2, {})} | custom-call | tf_op jit(solution)/shard_map/pallas_call | solution.py:35
  46.2 0.7 %copy.17 = f32[256,256]{1,0:T(8,128)} copy(f32[256,256]{1,0:T(8,128)S(1)} %get-tuple-element.37) | data formatting | bytes 524288
  46.9 1.9 %shard_map.54 = (f32[256,512]{1,0:T(8,128)}, f32[256,512]{1,0:T(8,128)}) custom-call(f32[256,256]{1,0:T(8,128)S(1)} %get-tuple-element.30.w_ref, f32[256,256]{1,0:T(8,128)S(1)} %add.23.mine_ref, f32[256,256]{1,0:T(8,128)S(1)} %collective-permute-done.10.other_ref, f32[256,256]{1,0:T(8,128)S(1)} %get-tuple-element.31.panel_ref, ...), custom_call_target="tpu_custom_call" | custom-call | tf_op jit(solution)/shard_map/pallas_call | solution.py:35
  (12 shorter events, 0.4 us)
Async XLA Ops:
  0.6 7.7 %collective-permute-start = (f32[64,256]{1,0:T(8,128)}, f32[64,256]{1,0:T(8,128)S(1)}, u32[]{:S(2)}, u32[]{:S(2)}) collective-permute-start(f32[64,256]{1,0:T(8,128)} %panel_hbm.1), channel_id=1, source_target_pairs={{0,1},{1,2},{2,3},{3,0},{4,5},{5,6},{6,7},{7,4},{8,9},{9,10},{10,1... | collective-permute-start | bytes 196616 | tf_op jit(solution)/shard_map/ppermute | solution.py:240
  3.7 5.2 %collective-permute-start.2 = (f32[64,256]{1,0:T(8,128)}, f32[64,256]{1,0:T(8,128)S(1)}, u32[]{:S(2)}, u32[]{:S(2)}) collective-permute-start(f32[64,256]{1,0:T(8,128)} %panel_hbm.1), channel_id=1, source_target_pairs={{0,3},{1,0},{2,1},{3,2},{4,7},{5,4},{6,5},{7,6},{8,11},{9,8},{10,9... | collective-permute-start | bytes 196616 | tf_op jit(solution)/shard_map/ppermute | solution.py:240
  5.8 6.4 %collective-permute-start.1 = (f32[64,256]{1,0:T(8,128)}, f32[64,256]{1,0:T(8,128)S(1)}, u32[]{:S(2)}, u32[]{:S(2)}) collective-permute-start(f32[64,256]{1,0:T(8,128)} %panel_hbm.1), channel_id=1, source_target_pairs={{0,2},{1,3},{2,0},{3,1},{4,6},{5,7},{6,4},{7,5},{8,10},{9,11},{10,... | collective-permute-start | bytes 196616 | tf_op jit(solution)/shard_map/ppermute | solution.py:240
  13.1 1.6 %collective-permute-start.7 = (f32[256,256]{1,0:T(8,128)S(1)}, f32[256,256]{1,0:T(8,128)S(1)}, u32[]{:S(2)}, u32[]{:S(2)}) collective-permute-start(f32[256,256]{1,0:T(8,128)S(1)} %get-tuple-element.34), channel_id=1, source_target_pairs={{0,4},{4,0},{8,12},{12,8},{16,20},{20,16},{24,28},{28,24},{1,5},{5... | collective-permute-start | bytes 786440 | tf_op jit(solution)/shard_map/ppermute | solution.py:240
  14.7 6.4 %collective-permute-start.8 = (f32[256,256]{1,0:T(8,128)S(1)}, f32[256,256]{1,0:T(8,128)S(1)}, u32[]{:S(2)}, u32[]{:S(2)}) collective-permute-start(f32[256,256]{1,0:T(8,128)S(1)} %add.21), channel_id=1, source_target_pairs={{0,8},{4,20},{8,0},{12,28},{16,24},{20,4},{24,16},{28,12},{1,9},{5... | collective-permute-start | bytes 786440 | tf_op jit(solution)/shard_map/ppermute | solution.py:240
  21.2 6.4 %collective-permute-start.9 = (f32[256,256]{1,0:T(8,128)S(1)}, f32[256,256]{1,0:T(8,128)S(1)}, u32[]{:S(2)}, u32[]{:S(2)}) collective-permute-start(f32[256,256]{1,0:T(8,128)S(1)} %add.22), channel_id=1, source_target_pairs={{0,16},{4,12},{8,24},{12,4},{16,0},{20,28},{24,8},{28,20},{1,17},{... | collective-permute-start | bytes 786440 | tf_op jit(solution)/shard_map/ppermute | solution.py:240
  22.8 5.0 %collective-permute-start.3 = (f32[136,128]{1,0:T(8,128)S(1)}, f32[136,128]{1,0:T(8,128)S(1)}, u32[]{:S(2)}, u32[]{:S(2)}) collective-permute-start(f32[136,128]{1,0:T(8,128)S(1)} %get-tuple-element.22), channel_id=1, source_target_pairs={{0,4},{4,0},{8,12},{12,8},{16,20},{20,16},{24,28},{28,24},{1,5},{5... | collective-permute-start | bytes 208904 | tf_op jit(solution)/shard_map/ppermute | solution.py:240
  27.6 19.2 %collective-permute-start.10 = (f32[256,256]{1,0:T(8,128)S(1)}, f32[256,256]{1,0:T(8,128)S(1)}, u32[]{:S(2)}, u32[]{:S(2)}) collective-permute-start(f32[256,256]{1,0:T(8,128)S(1)} %add.23.mine_ref), channel_id=1, source_target_pairs={{0,4},{4,0},{8,12},{12,8},{16,20},{20,16},{24,28},{28,24},{1,5},{5... | collective-permute-start | bytes 786440 | tf_op jit(solution)/shard_map/ppermute | solution.py:240
  27.8 4.4 %collective-permute-start.4 = (f32[136,128]{1,0:T(8,128)S(1)}, f32[136,128]{1,0:T(8,128)S(1)}, u32[]{:S(2)}, u32[]{:S(2)}) collective-permute-start(f32[136,128]{1,0:T(8,128)S(1)} %add.18), channel_id=1, source_target_pairs={{0,8},{4,20},{8,0},{12,28},{16,24},{20,4},{24,16},{28,12},{1,9},{5... | collective-permute-start | bytes 208904 | tf_op jit(solution)/shard_map/ppermute | solution.py:240
  32.1 4.4 %collective-permute-start.5 = (f32[136,128]{1,0:T(8,128)S(1)}, f32[136,128]{1,0:T(8,128)S(1)}, u32[]{:S(2)}, u32[]{:S(2)}) collective-permute-start(f32[136,128]{1,0:T(8,128)S(1)} %add.19), channel_id=1, source_target_pairs={{0,16},{4,12},{8,24},{12,4},{16,0},{20,28},{24,8},{28,20},{1,17},{... | collective-permute-start | bytes 208904 | tf_op jit(solution)/shard_map/ppermute | solution.py:240
  36.5 1.3 %collective-permute-start.6 = (f32[136,128]{1,0:T(8,128)S(1)}, f32[136,128]{1,0:T(8,128)S(1)}, u32[]{:S(2)}, u32[]{:S(2)}) collective-permute-start(f32[136,128]{1,0:T(8,128)S(1)} %add.20.mine_ref), channel_id=1, source_target_pairs={{0,4},{4,0},{8,12},{12,8},{16,20},{20,16},{24,28},{28,24},{1,5},{5... | collective-permute-start | bytes 208904 | tf_op jit(solution)/shard_map/ppermute | solution.py:240

commit v3 on v2

--- a/solution.py
+++ b/solution.py
@@ -52,7 +52,7 @@
     half = width // 2
     here = lax.axis_index("cols")
     for step in range(count):
-        at = lax.rem(here - step + count, count)
+        at = here ^ step
         panel_ref[pl.ds(pl.multiple_of(at * height, height), height), :] = pieces[step][...]
     block = panel_ref[...]
     gram = product(block, block, 0, 0)
@@ -107,39 +107,37 @@
     return jnp.broadcast_to(x[:, c : c + 1], (x.shape[0], LANES))
 
 
-def factor_rows(rows, unit, tile, lane0):
+def factor_rows(rows, unit, tile, lane0, zero):
     groups, tiles = len(rows), len(rows[0])
     sub = lax.broadcasted_iota(jnp.int32, (SUBLANES, LANES), 0)
     for j in range(groups):
         own = rows[j] + [unit[j]]
-        out = list(own)
         col = {
             g: [along_lanes(rows[g][tile], lane0 + SUBLANES * j + c) for c in range(SUBLANES)] for g in range(j, groups)
         }
-        pivot = {(r, c): along_sublanes(col[j][c], r) for c in range(SUBLANES) for r in range(c, SUBLANES)}
-        low, done = {}, []
+        head = [x - zero for x in col[j]]
+        pivot = {(r, c): along_sublanes(head[c], r) for c in range(SUBLANES) for r in range(c, SUBLANES)}
+        low, done, scales = {}, [], zero
         for i in range(SUBLANES):
             scale = lax.rsqrt(pivot[i, i])
+            scales = jnp.where(sub == i, scale, scales)
+            below = zero
             for r in range(i + 1, SUBLANES):
                 low[r, i] = pivot[r, i] * scale
+                below = jnp.where(sub == r, low[r, i], below)
             for c in range(i + 1, SUBLANES):
                 for r in range(c, SUBLANES):
                     pivot[r, c] = pivot[r, c] - low[r, i] * low[c, i]
-            solved = []
-            for t in range(tiles + 1):
-                x = along_sublanes(own[t], i)
-                for m in range(i):
-                    x = x - low[i, m] * done[m][t]
-                x = x * scale
-                solved.append(x)
-                out[t] = jnp.where(sub == i, x, out[t])
-            done.append(solved)
+            done.append([along_sublanes(x, i) * scale for x in own])
+            if i + 1 < SUBLANES:
+                own = [x - below * y for x, y in zip(own, done[i])]
             for g in range(j + 1, groups):
                 x = col[g][i]
                 for m in range(i):
                     x = x - col[g][m] * low[i, m]
                 col[g][i] = x * scale
-        rows[j], unit[j] = out[:tiles], out[tiles]
+        own = [x * scales for x in own]
+        rows[j], unit[j] = own[:tiles], own[tiles]
         for g in range(j + 1, groups):
             for i in range(SUBLANES):
                 for t in range(tiles):
@@ -147,7 +145,7 @@
                 unit[g] = unit[g] - col[g][i] * done[i][tiles]
 
 
-def factor_block(m_ref, r_ref, w_ref, k):
+def factor_block(m_ref, r_ref, w_ref, zero_ref, k):
     n = m_ref.shape[0]
     tiles, groups = n // LANES, BLOCK // SUBLANES
     sub = lax.broadcasted_iota(jnp.int32, (SUBLANES, LANES), 0)
@@ -158,7 +156,7 @@
     at = lambda g, t: (slice(base + SUBLANES * g, base + SUBLANES * (g + 1)), slice(LANES * t, LANES * (t + 1)))
     rows = [[m_ref[at(g, t)] for t in range(tiles)] for g in range(groups)]
     unit = [jnp.where(lane == lane0 + SUBLANES * g + sub, 1.0, 0.0).astype(jnp.float32) for g in range(groups)]
-    factor_rows(rows, unit, tile, lane0)
+    factor_rows(rows, unit, tile, lane0, zero_ref[...])
     inside = (lane >= lane0) & (lane < lane0 + BLOCK)
     both = [[jnp.where(inside, unit[g], rows[g][t]) if t == tile else rows[g][t] for t in range(tiles)] for g in range(groups)]
     for g in range(groups):
@@ -177,15 +175,17 @@
         m_ref[below:, :] = jnp.where((c >= base) & (c < below), 0.0, old) - change
 
 
-def factor_first_kernel(mine_ref, other_ref, m_ref, r_ref, w_ref, *, stop):
+def factor_first_kernel(mine_ref, other_ref, m_ref, r_ref, w_ref, zero_ref, *, stop):
+    zero_ref[...] = jnp.zeros_like(zero_ref)
     unpack(mine_ref, other_ref, m_ref)
     for k in range(stop):
-        factor_block(m_ref, r_ref, w_ref, k)
-
-
-def factor_more_kernel(m0_ref, r0_ref, w0_ref, m_ref, r_ref, w_ref, *, start, stop):
+        factor_block(m_ref, r_ref, w_ref, zero_ref, k)
+
+
+def factor_more_kernel(m0_ref, r0_ref, w0_ref, m_ref, r_ref, w_ref, zero_ref, *, start, stop):
+    zero_ref[...] = jnp.zeros_like(zero_ref)
     for k in range(start, stop):
-        factor_block(m_ref, r_ref, w_ref, k)
+        factor_block(m_ref, r_ref, w_ref, zero_ref, k)
 
 
 def cross_kernel(panel_ref, trailing_ref, keep_ref, send_ref):
@@ -204,15 +204,19 @@
         send_ref[...] = terms[:, :half]
 
 
-def finish_kernel(w_ref, mine_ref, other_ref, panel_ref, trailing_ref, coefficients_ref, updated_ref, c_ref, u_ref, sems):
+def finish_kernel(
+    r_ref, w_ref, mine_ref, other_ref, panel_ref, trailing_ref, factor_ref, coefficients_ref, updated_ref, c_ref, u_ref, sems
+):
+    copies = [pltpu.make_async_copy(r_ref, factor_ref, sems.at[1 + PARTS])]
+    copies[0].start()
     inverse = w_ref[...]
     even = lax.rem(lax.axis_index("rows"), 2) == 0
     mine, other = mine_ref[...], other_ref[...]
     terms = jnp.concatenate([jnp.where(even, mine, other), jnp.where(even, other, mine)], axis=1)
     coefficients = product(inverse, terms, 1, 0)
     c_ref[...] = coefficients
-    copies = [pltpu.make_async_copy(c_ref, coefficients_ref, sems.at[0])]
-    copies[0].start()
+    copies.append(pltpu.make_async_copy(c_ref, coefficients_ref, sems.at[0]))
+    copies[-1].start()
     basis = product(panel_ref[...], inverse, 1, 1)
     tall = u_ref.shape[0] // PARTS
     for part in range(PARTS):
@@ -222,6 +226,10 @@
         copies[-1].start()
     for copy in copies:
         copy.wait()
+
+
+def gather_steps(n_cols):
+    return [*range(n_cols // 2, n_cols), *range(1, n_cols // 2)]
 
 
 def local(panel, trailing, *, n_rows, n_cols):
@@ -252,8 +260,9 @@
         name="stage",
     )(panel, trailing)
     pieces = [panel_here]
-    for step in range(1, n_cols):
-        pieces.append(sent(panel, [(i, (i + step) % n_cols) for i in range(n_cols)], "cols"))
+    steps = gather_steps(n_cols)
+    got = {step: sent(panel, [(i, i ^ step) for i in range(n_cols)], "cols") for step in steps}
+    pieces += [got[step] for step in range(1, n_cols)]
     packed, square = (half + SUBLANES, half), (width, width)
     panel_block, g, g_send = call(
         functools.partial(gram_kernel, count=n_cols), [(tall, width), packed, packed], *pieces
@@ -265,46 +274,46 @@
     for pairs in rounds:
         g = summed(g, pairs)
     g_other = sent(g, partner)
-    for pairs in rounds[:-1]:
+    for pairs in rounds:
         c = summed(c, pairs)
     blocks = width // BLOCK
-    cuts = [blocks * 3 // 8, blocks * 7 // 8, blocks]
-    state = call(functools.partial(factor_first_kernel, stop=cuts[0]), [square] * 3, g, g_other)
-    c = summed(c, rounds[-1])
-    for i in (1, 2):
+    zero = [pltpu.VMEM((SUBLANES, LANES), jnp.float32)]
+    cuts = [blocks * 7 // 8, blocks]
+    state = call(functools.partial(factor_first_kernel, stop=cuts[0]), [square] * 3, g, g_other, scratch_shapes=zero)
+    c_other = sent(c, partner)
+    for i in (1,):
         state = call(
             functools.partial(factor_more_kernel, start=cuts[i - 1], stop=cuts[i]),
             [square] * 3,
             *state,
+            scratch_shapes=zero,
             aliases={0: 0, 1: 1, 2: 2},
         )
-        if i == 1:
-            c_other = sent(c, partner)
     _, r, w = state
     hbm = pl.BlockSpec(memory_space=pl.ANY)
-    coefficients, updated = call(
+    return call(
         finish_kernel,
-        [(width, wide), (tall, wide)],
+        [square, (width, wide), (tall, wide)],
+        r,
         w,
         c,
         c_other,
         panel_block,
         trailing,
         in_vmem=False,
-        out_specs=[hbm, hbm],
+        out_specs=[hbm] * 3,
         scratch_shapes=[
             pltpu.VMEM((width, wide), jnp.float32),
             pltpu.VMEM((tall, wide), jnp.float32),
-            pltpu.SemaphoreType.DMA((1 + PARTS,)),
+            pltpu.SemaphoreType.DMA((2 + PARTS,)),
         ],
     )
-    return r, coefficients, updated
 
 
 def solution(mesh):
-    n_rows = mesh.shape["rows"]
+    n_rows, n_cols = mesh.shape["rows"], mesh.shape["cols"]
     return jax.shard_map(
-        functools.partial(local, n_rows=n_rows, n_cols=mesh.shape["cols"]),
+        functools.partial(local, n_rows=n_rows, n_cols=n_cols),
         mesh=mesh,
         in_specs=(P(("rows", "cols"), None), P("rows", "cols")),
         out_specs=(P(), P(None, "cols"), P("rows", "cols")),

time: 48.9 us -> 47.3 us (0.967)
  Pallas kernels: 12 us -> 10.5 us
  waiting for transfers between devices: 22.5 us -> 23.6 us
  local copies, waits for them, and re-layouts: 0.71 us -> 0 us
  starting transfers between devices: 12.7 us -> 12.2 us
    pallas_call x6 -> x5, Pallas kernels: 10.9 us -> 9.37 us  [call(): pl.pallas_call(body, out_shape=shapes, input_output_aliases=aliases or {}...]
    ppermute x11, waiting for transfers between devices: 22.5 us -> 23.6 us  [sent(): return lax.ppermute(x, axis, pairs)]
    unnamed x1 -> x0, local copies, waits for them, and re-layouts: 0.71 us -> none
  transfers between devices with their start and end apart: 11 -> 11, of which waited for: 9 -> 8; matrix products, arithmetic and copies ran while one was open for 2% -> 0% of each run, Pallas kernels for 19% -> 17%
where the time goes in v3:
time: 47.3 us; the launch traced here: 47.1 us
  waiting for transfers between devices  23.6 us (50%)
  starting transfers between devices  12.2 us (26%)
  Pallas kernels  10.5 us (22%)
  between operations  0.74 us (2%)
    ppermute x11, waiting for transfers between devices, sent(): return lax.ppermute(x, axis, pairs)  23.6 us
    ppermute x11, starting transfers between devices, sent(): return lax.ppermute(x, axis, pairs)  12.2 us
    pallas_call x5, Pallas kernels, call(): pl.pallas_call(body, out_shape=shapes, input_output_aliases=aliases or {}...  9.37 us
    pallas_call x1, Pallas kernels, local(): pl.pallas_call(stage_kernel, out_shape=[pltpu.VMEM(x.shape, x.dtype) for...  1.1 us
  transfers between devices with their start and end apart: 11, of which 8 were waited for; matrix products, arithmetic and copies ran while one was open for 0% of the time, Pallas kernels for 17%

profile of v3, /device:TPU:0, one launch (start us, length us, event | category | flops | bytes accessed | tf_op | source)
XLA Modules:
  0.0 47.1 jit_solution(15614162368860213743)
XLA Ops:
  0.6 3.1 %collective-permute-start = (f32[64,256]{1,0:T(8,128)}, f32[64,256]{1,0:T(8,128)S(1)}, u32[]{:S(2)}, u32[]{:S(2)}) collective-permute-start(f32[64,256]{1,0:T(8,128)} %panel_hbm.1), channel_id=1, source_target_pairs={{0,1},{1,0},{2,3},{3,2},{4,5},{5,4},{6,7},{7,6},{8,9},{9,8},{10,11... | collective-permute-start | bytes 196616 | tf_op jit(solution)/shard_map/ppermute | solution.py:248
  3.7 2.5 %collective-permute-start.2 = (f32[64,256]{1,0:T(8,128)}, f32[64,256]{1,0:T(8,128)S(1)}, u32[]{:S(2)}, u32[]{:S(2)}) collective-permute-start(f32[64,256]{1,0:T(8,128)} %panel_hbm.1), channel_id=1, source_target_pairs={{0,3},{1,2},{2,1},{3,0},{4,7},{5,6},{6,5},{7,4},{8,11},{9,10},{10,... | collective-permute-start | bytes 196616 | tf_op jit(solution)/shard_map/ppermute | solution.py:248
  6.2 0.1 collective-permute-start.1
  6.3 1.1 %stage.1 = (f32[64,256]{1,0:T(8,128)S(1)}, f32[256,512]{1,0:T(8,128)S(1)}) custom-call(f32[64,256]{1,0:T(8,128)} %panel_hbm.1, f32[256,512]{1,0:T(8,128)} %trailing_hbm.1), custom_call_target="tpu_custom_call" | custom-call | tf_op jit(solution)/shard_map/stage/pallas_call | solution.py:254
  7.5 3.4 %collective-permute-done.2.refs_3_ = f32[64,256]{1,0:T(8,128)S(1)} collective-permute-done((f32[64,256]{1,0:T(8,128)}, f32[64,256]{1,0:T(8,128)S(1)}, u32[]{:S(2)}, u32[]{:S(2)}) %collective-permute-start.2) | collective-permute-done | bytes 65568 | tf_op jit(solution)/shard_map/ppermute | solution.py:248
  10.8 2.1 %collective-permute-done.1.refs_2_ = f32[64,256]{1,0:T(8,128)S(1)} collective-permute-done((f32[64,256]{1,0:T(8,128)}, f32[64,256]{1,0:T(8,128)S(1)}, u32[]{:S(2)}, u32[]{:S(2)}) %collective-permute-start.1) | collective-permute-done | bytes 65568 | tf_op jit(solution)/shard_map/ppermute | solution.py:248
  12.9 0.3 shard_map.49
  13.2 0.4 shard_map.52
  13.7 0.1 collective-permute-start.7
  13.8 1.5 %collective-permute-done.7 = f32[256,256]{1,0:T(8,128)S(1)} collective-permute-done((f32[256,256]{1,0:T(8,128)S(1)}, f32[256,256]{1,0:T(8,128)S(1)}, u32[]{:S(2)}, u32[]{:S(2)}) %collective-permute-start.7) | collective-permute-done | bytes 262176 | tf_op jit(solution)/shard_map/ppermute | solution.py:248
  15.3 1.6 %collective-permute-start.8 = (f32[256,256]{1,0:T(8,128)S(1)}, f32[256,256]{1,0:T(8,128)S(1)}, u32[]{:S(2)}, u32[]{:S(2)}) collective-permute-start(f32[256,256]{1,0:T(8,128)S(1)} %add.21), channel_id=1, source_target_pairs={{0,8},{4,20},{8,0},{12,28},{16,24},{20,4},{24,16},{28,12},{1,9},{5... | collective-permute-start | bytes 786440 | tf_op jit(solution)/shard_map/ppermute | solution.py:248
  16.9 4.9 %collective-permute-done.8 = f32[256,256]{1,0:T(8,128)S(1)} collective-permute-done((f32[256,256]{1,0:T(8,128)S(1)}, f32[256,256]{1,0:T(8,128)S(1)}, u32[]{:S(2)}, u32[]{:S(2)}) %collective-permute-start.8) | collective-permute-done | bytes 262176 | tf_op jit(solution)/shard_map/ppermute | solution.py:248
  21.8 1.6 %collective-permute-start.9 = (f32[256,256]{1,0:T(8,128)S(1)}, f32[256,256]{1,0:T(8,128)S(1)}, u32[]{:S(2)}, u32[]{:S(2)}) collective-permute-start(f32[256,256]{1,0:T(8,128)S(1)} %add.22), channel_id=1, source_target_pairs={{0,16},{4,12},{8,24},{12,4},{16,0},{20,28},{24,8},{28,20},{1,17},{... | collective-permute-start | bytes 786440 | tf_op jit(solution)/shard_map/ppermute | solution.py:248
  23.4 4.9 %collective-permute-done.9 = f32[256,256]{1,0:T(8,128)S(1)} collective-permute-done((f32[256,256]{1,0:T(8,128)S(1)}, f32[256,256]{1,0:T(8,128)S(1)}, u32[]{:S(2)}, u32[]{:S(2)}) %collective-permute-start.9) | collective-permute-done | bytes 262176 | tf_op jit(solution)/shard_map/ppermute | solution.py:248
  28.3 0.1 collective-permute-start.10
  28.4 1.6 %collective-permute-start.4 = (f32[136,128]{1,0:T(8,128)S(1)}, f32[136,128]{1,0:T(8,128)S(1)}, u32[]{:S(2)}, u32[]{:S(2)}) collective-permute-start(f32[136,128]{1,0:T(8,128)S(1)} %add.18), channel_id=1, source_target_pairs={{0,8},{4,20},{8,0},{12,28},{16,24},{20,4},{24,16},{28,12},{1,9},{5... | collective-permute-start | bytes 208904 | tf_op jit(solution)/shard_map/ppermute | solution.py:248
  29.9 2.8 %collective-permute-done.4 = f32[136,128]{1,0:T(8,128)S(1)} collective-permute-done((f32[136,128]{1,0:T(8,128)S(1)}, f32[136,128]{1,0:T(8,128)S(1)}, u32[]{:S(2)}, u32[]{:S(2)}) %collective-permute-start.4) | collective-permute-done | bytes 69664 | tf_op jit(solution)/shard_map/ppermute | solution.py:248
  32.8 1.6 %collective-permute-start.5 = (f32[136,128]{1,0:T(8,128)S(1)}, f32[136,128]{1,0:T(8,128)S(1)}, u32[]{:S(2)}, u32[]{:S(2)}) collective-permute-start(f32[136,128]{1,0:T(8,128)S(1)} %add.19), channel_id=1, source_target_pairs={{0,16},{4,12},{8,24},{12,4},{16,0},{20,28},{24,8},{28,20},{1,17},{... | collective-permute-start | bytes 208904 | tf_op jit(solution)/shard_map/ppermute | solution.py:248
  34.3 2.8 %collective-permute-done.5 = f32[136,128]{1,0:T(8,128)S(1)} collective-permute-done((f32[136,128]{1,0:T(8,128)S(1)}, f32[136,128]{1,0:T(8,128)S(1)}, u32[]{:S(2)}, u32[]{:S(2)}) %collective-permute-start.5) | collective-permute-done | bytes 69664 | tf_op jit(solution)/shard_map/ppermute | solution.py:248
  37.2 0.1 collective-permute-start.6
  37.2 1.2 %collective-permute-done.6.other_ref = f32[136,128]{1,0:T(8,128)S(1)} collective-permute-done((f32[136,128]{1,0:T(8,128)S(1)}, f32[136,128]{1,0:T(8,128)S(1)}, u32[]{:S(2)}, u32[]{:S(2)}) %collective-permute-start.6) | collective-permute-done | bytes 69664 | tf_op jit(solution)/shard_map/ppermute | solution.py:248
  38.5 6.1 %shard_map.50 = (f32[256,256]{1,0:T(8,128)S(1)}, f32[256,256]{1,0:T(8,128)S(1)}, f32[256,256]{1,0:T(8,128)S(1)}) custom-call(f32[136,128]{1,0:T(8,128)S(1)} %add.20.mine_ref, f32[136,128]{1,0:T(8,128)S(1)} %collective-permute-done.6.other_ref), custom_call_target="tpu_custom_call" | custom-call | tf_op jit(solution)/shard_map/pallas_call | solution.py:35
  44.6 0.6 %shard_map.51 = (f32[256,256]{1,0:T(8,128)S(1)}, f32[256,256]{1,0:T(8,128)S(1)}, f32[256,256]{1,0:T(8,128)S(1)}) custom-call(f32[256,256]{1,0:T(8,128)S(1)} %get-tuple-element.18.m0_ref, f32[256,256]{1,0:T(8,128)S(1)} %get-tuple-element.19.r0_ref, f32[256,256]{1,0:T(8,128)S(1)} %get-tuple-element.20.w0_ref), custom_call_target="tpu_custom_call", output_to_operand_aliasing={{0}: (0, {}), {1}: (1, {}), {2}: (2, {})} | custom-call | tf_op jit(solution)/shard_map/pallas_call | solution.py:35
  45.2 1.9 %shard_map.53 = (f32[256,256]{1,0:T(8,128)}, f32[256,512]{1,0:T(8,128)}, f32[256,512]{1,0:T(8,128)}) custom-call(f32[256,256]{1,0:T(8,128)S(1)} %get-tuple-element.21.r_ref, f32[256,256]{1,0:T(8,128)S(1)} %get-tuple-element.22.w_ref, f32[256,256]{1,0:T(8,128)S(1)} %add.23.mine_ref, f32[256,256]{1,0:T(8,128)S(1)} %collective-permute-done.10.other_ref, ...), custom_call_target="tpu_custom_call" | custom-call | tf_op jit(solution)/shard_map/pallas_call | solution.py:35
  (10 shorter events, 0.1 us)
Async XLA Ops:
  0.6 6.8 %collective-permute-start = (f32[64,256]{1,0:T(8,128)}, f32[64,256]{1,0:T(8,128)S(1)}, u32[]{:S(2)}, u32[]{:S(2)}) collective-permute-start(f32[64,256]{1,0:T(8,128)} %panel_hbm.1), channel_id=1, source_target_pairs={{0,1},{1,0},{2,3},{3,2},{4,5},{5,4},{6,7},{7,6},{8,9},{9,8},{10,11... | collective-permute-start | bytes 196616 | tf_op jit(solution)/shard_map/ppermute | solution.py:248
  3.7 7.1 %collective-permute-start.2 = (f32[64,256]{1,0:T(8,128)}, f32[64,256]{1,0:T(8,128)S(1)}, u32[]{:S(2)}, u32[]{:S(2)}) collective-permute-start(f32[64,256]{1,0:T(8,128)} %panel_hbm.1), channel_id=1, source_target_pairs={{0,3},{1,2},{2,1},{3,0},{4,7},{5,6},{6,5},{7,4},{8,11},{9,10},{10,... | collective-permute-start | bytes 196616 | tf_op jit(solution)/shard_map/ppermute | solution.py:248
  6.2 6.7 %collective-permute-start.1 = (f32[64,256]{1,0:T(8,128)}, f32[64,256]{1,0:T(8,128)S(1)}, u32[]{:S(2)}, u32[]{:S(2)}) collective-permute-start(f32[64,256]{1,0:T(8,128)} %panel_hbm.1), channel_id=1, source_target_pairs={{0,2},{1,3},{2,0},{3,1},{4,6},{5,7},{6,4},{7,5},{8,10},{9,11},{10,... | collective-permute-start | bytes 196616 | tf_op jit(solution)/shard_map/ppermute | solution.py:248
  13.7 1.6 %collective-permute-start.7 = (f32[256,256]{1,0:T(8,128)S(1)}, f32[256,256]{1,0:T(8,128)S(1)}, u32[]{:S(2)}, u32[]{:S(2)}) collective-permute-start(f32[256,256]{1,0:T(8,128)S(1)} %get-tuple-element.26), channel_id=1, source_target_pairs={{0,4},{4,0},{8,12},{12,8},{16,20},{20,16},{24,28},{28,24},{1,5},{5... | collective-permute-start | bytes 786440 | tf_op jit(solution)/shard_map/ppermute | solution.py:248
  15.3 6.4 %collective-permute-start.8 = (f32[256,256]{1,0:T(8,128)S(1)}, f32[256,256]{1,0:T(8,128)S(1)}, u32[]{:S(2)}, u32[]{:S(2)}) collective-permute-start(f32[256,256]{1,0:T(8,128)S(1)} %add.21), channel_id=1, source_target_pairs={{0,8},{4,20},{8,0},{12,28},{16,24},{20,4},{24,16},{28,12},{1,9},{5... | collective-permute-start | bytes 786440 | tf_op jit(solution)/shard_map/ppermute | solution.py:248
  21.8 6.4 %collective-permute-start.9 = (f32[256,256]{1,0:T(8,128)S(1)}, f32[256,256]{1,0:T(8,128)S(1)}, u32[]{:S(2)}, u32[]{:S(2)}) collective-permute-start(f32[256,256]{1,0:T(8,128)S(1)} %add.22), channel_id=1, source_target_pairs={{0,16},{4,12},{8,24},{12,4},{16,0},{20,28},{24,8},{28,20},{1,17},{... | collective-permute-start | bytes 786440 | tf_op jit(solution)/shard_map/ppermute | solution.py:248
  23.4 5.0 %collective-permute-start.3 = (f32[136,128]{1,0:T(8,128)S(1)}, f32[136,128]{1,0:T(8,128)S(1)}, u32[]{:S(2)}, u32[]{:S(2)}) collective-permute-start(f32[136,128]{1,0:T(8,128)S(1)} %get-tuple-element.17), channel_id=1, source_target_pairs={{0,4},{4,0},{8,12},{12,8},{16,20},{20,16},{24,28},{28,24},{1,5},{5... | collective-permute-start | bytes 208904 | tf_op jit(solution)/shard_map/ppermute | solution.py:248
  28.3 17.0 %collective-permute-start.10 = (f32[256,256]{1,0:T(8,128)S(1)}, f32[256,256]{1,0:T(8,128)S(1)}, u32[]{:S(2)}, u32[]{:S(2)}) collective-permute-start(f32[256,256]{1,0:T(8,128)S(1)} %add.23.mine_ref), channel_id=1, source_target_pairs={{0,4},{4,0},{8,12},{12,8},{16,20},{20,16},{24,28},{28,24},{1,5},{5... | collective-permute-start | bytes 786440 | tf_op jit(solution)/shard_map/ppermute | solution.py:248
  28.4 4.4 %collective-permute-start.4 = (f32[136,128]{1,0:T(8,128)S(1)}, f32[136,128]{1,0:T(8,128)S(1)}, u32[]{:S(2)}, u32[]{:S(2)}) collective-permute-start(f32[136,128]{1,0:T(8,128)S(1)} %add.18), channel_id=1, source_target_pairs={{0,8},{4,20},{8,0},{12,28},{16,24},{20,4},{24,16},{28,12},{1,9},{5... | collective-permute-start | bytes 208904 | tf_op jit(solution)/shard_map/ppermute | solution.py:248
  32.8 4.4 %collective-permute-start.5 = (f32[136,128]{1,0:T(8,128)S(1)}, f32[136,128]{1,0:T(8,128)S(1)}, u32[]{:S(2)}, u32[]{:S(2)}) collective-permute-start(f32[136,128]{1,0:T(8,128)S(1)} %add.19), channel_id=1, source_target_pairs={{0,16},{4,12},{8,24},{12,4},{16,0},{20,28},{24,8},{28,20},{1,17},{... | collective-permute-start | bytes 208904 | tf_op jit(solution)/shard_map/ppermute | solution.py:248
  37.2 1.3 %collective-permute-start.6 = (f32[136,128]{1,0:T(8,128)S(1)}, f32[136,128]{1,0:T(8,128)S(1)}, u32[]{:S(2)}, u32[]{:S(2)}) collective-permute-start(f32[136,128]{1,0:T(8,128)S(1)} %add.20.mine_ref), channel_id=1, source_target_pairs={{0,4},{4,0},{8,12},{12,8},{16,20},{20,16},{24,28},{28,24},{1,5},{5... | collective-permute-start | bytes 208904 | tf_op jit(solution)/shard_map/ppermute | solution.py:248

commit v4 on v3

--- a/solution.py
+++ b/solution.py
@@ -8,7 +8,9 @@
 from jax.sharding import PartitionSpec as P
 
 
-LANES, SUBLANES, BLOCK, PARTS = 128, 8, 32, 4
+LANES, SUBLANES, BLOCK, INNER, PARTS = 128, 8, 32, 4, 4
+
+SMALL = pltpu.CompilerParams(vmem_limit_bytes=16 << 20)
 
 
 def split(x):
@@ -31,7 +33,7 @@
     block = pl.BlockSpec(memory_space=pltpu.VMEM)
     shapes = [(pltpu.VMEM if in_vmem else jax.ShapeDtypeStruct)(s, jnp.float32) for s in outs]
     args = [pltpu.with_memory_space_constraint(x, pltpu.VMEM) for x in args]
-    extra = {"in_specs": [block] * len(args), "out_specs": [block] * len(outs)} | extra
+    extra = {"in_specs": [block] * len(args), "out_specs": [block] * len(outs), "compiler_params": SMALL} | extra
     return pl.pallas_call(body, out_shape=shapes, input_output_aliases=aliases or {}, **extra)(*args)
 
 
@@ -112,30 +114,51 @@
     sub = lax.broadcasted_iota(jnp.int32, (SUBLANES, LANES), 0)
     for j in range(groups):
         own = rows[j] + [unit[j]]
-        col = {
-            g: [along_lanes(rows[g][tile], lane0 + SUBLANES * j + c) for c in range(SUBLANES)] for g in range(j, groups)
+        spread = lambda step: {
+            g: [along_lanes(rows[g][tile], lane0 + SUBLANES * step + c) for c in range(SUBLANES)]
+            for g in range(step, groups)
         }
-        head = [x - zero for x in col[j]]
-        pivot = {(r, c): along_sublanes(head[c], r) for c in range(SUBLANES) for r in range(c, SUBLANES)}
-        low, done, scales = {}, [], zero
+        if j == 0:
+            col = spread(0)
+            col[0] = [x - zero for x in col[0]]
+        else:
+            col = following
+        following = spread(j + 1)
+        head = list(col[j])
+        low, ours, done, scales = {}, [], [], zero
         for i in range(SUBLANES):
+            start = i - i % INNER
+            stop = start + INNER
+            if i == start:
+                for c in range(i, SUBLANES):
+                    for m in range(max(start - INNER, 0), start):
+                        low[c, m] = along_sublanes(ours[m], c)
+                        head[c] = head[c] - ours[m] * low[c, m]
+                pivot = {(r, c): along_sublanes(head[c], r) for c in range(i, stop) for r in range(c, stop)}
             scale = lax.rsqrt(pivot[i, i])
             scales = jnp.where(sub == i, scale, scales)
-            below = zero
-            for r in range(i + 1, SUBLANES):
+            for r in range(i + 1, stop):
                 low[r, i] = pivot[r, i] * scale
-                below = jnp.where(sub == r, low[r, i], below)
-            for c in range(i + 1, SUBLANES):
-                for r in range(c, SUBLANES):
+            for c in range(i + 1, stop):
+                for r in range(c, stop):
                     pivot[r, c] = pivot[r, c] - low[r, i] * low[c, i]
+            x = head[i]
+            for m in range(start, i):
+                x = x - ours[m] * low[i, m]
+            ours.append(x * scale)
             done.append([along_sublanes(x, i) * scale for x in own])
             if i + 1 < SUBLANES:
+                below = jnp.where(sub > i, ours[i], zero)
                 own = [x - below * y for x, y in zip(own, done[i])]
             for g in range(j + 1, groups):
                 x = col[g][i]
                 for m in range(i):
                     x = x - col[g][m] * low[i, m]
                 col[g][i] = x * scale
+            for c in range(SUBLANES if j + 1 < groups else 0):
+                factor = along_sublanes(col[j + 1][i], c)
+                for g in range(j + 1, groups):
+                    following[g][c] = following[g][c] - col[g][i] * factor
         own = [x * scales for x in own]
         rows[j], unit[j] = own[:tiles], own[tiles]
         for g in range(j + 1, groups):
@@ -175,17 +198,43 @@
         m_ref[below:, :] = jnp.where((c >= base) & (c < below), 0.0, old) - change
 
 
-def factor_first_kernel(mine_ref, other_ref, m_ref, r_ref, w_ref, zero_ref, *, stop):
+def factor_first_kernel(mine_ref, other_ref, m_ref, r_ref, w_ref, factor_ref, zero_ref, sem, *, stop):
     zero_ref[...] = jnp.zeros_like(zero_ref)
     unpack(mine_ref, other_ref, m_ref)
+    copies = []
     for k in range(stop):
         factor_block(m_ref, r_ref, w_ref, zero_ref, k)
-
-
-def factor_more_kernel(m0_ref, r0_ref, w0_ref, m_ref, r_ref, w_ref, zero_ref, *, start, stop):
+        if k + 1 < stop:
+            at = slice(k * BLOCK, (k + 1) * BLOCK)
+            copies.append(pltpu.make_async_copy(r_ref.at[at, :], factor_ref.at[at, :], sem.at[k]))
+            copies[-1].start()
+    for copy in copies:
+        copy.wait()
+
+
+def from_inverse(w_ref, x):
+    half = w_ref.shape[0] // 2
+    return product(w_ref[:half, :half], x[:half, :], 1, 0), product(w_ref[half:, :], x, 1, 0)
+
+
+def column_half(half, mine):
+    odd = lax.rem(lax.axis_index("rows"), 2)
+    return pl.ds(pl.multiple_of((odd if mine else 1 - odd) * half, LANES), half)
+
+
+def factor_last_kernel(
+    m0_ref, r0_ref, w0_ref, panel_ref, terms_ref, trailing_ref, m_ref, r_ref, w_ref, basis_ref, c_ref, u_ref, zero_ref, *, start, stop
+):
     zero_ref[...] = jnp.zeros_like(zero_ref)
     for k in range(start, stop):
         factor_block(m_ref, r_ref, w_ref, zero_ref, k)
+    half = w_ref.shape[0] // 2
+    basis_ref[:, :half] = product(panel_ref[:, :half], w_ref[:half, :half], 1, 1)
+    basis_ref[:, half:] = product(panel_ref[...], w_ref[half:, :], 1, 1)
+    coefficients = jnp.concatenate(from_inverse(w_ref, terms_ref[...]), axis=0)
+    c_ref[...] = coefficients
+    columns = column_half(c_ref.shape[1], True)
+    u_ref[...] = trailing_ref[:, columns] - product(basis_ref[...], coefficients, 1, 0)
 
 
 def cross_kernel(panel_ref, trailing_ref, keep_ref, send_ref):
@@ -204,26 +253,28 @@
         send_ref[...] = terms[:, :half]
 
 
-def finish_kernel(
-    r_ref, w_ref, mine_ref, other_ref, panel_ref, trailing_ref, factor_ref, coefficients_ref, updated_ref, c_ref, u_ref, sems
-):
-    copies = [pltpu.make_async_copy(r_ref, factor_ref, sems.at[1 + PARTS])]
-    copies[0].start()
-    inverse = w_ref[...]
-    even = lax.rem(lax.axis_index("rows"), 2) == 0
-    mine, other = mine_ref[...], other_ref[...]
-    terms = jnp.concatenate([jnp.where(even, mine, other), jnp.where(even, other, mine)], axis=1)
-    coefficients = product(inverse, terms, 1, 0)
+def finish_kernel(*refs, done):
+    r_ref, w_ref, basis_ref, mine_c_ref, mine_u_ref, terms_ref, trailing_ref, _, *outs, c_ref, u_ref, sems = refs
+    factor_ref, coefficients_ref, updated_ref = outs
+    _, wide = c_ref.shape
+    mine, other = column_half(wide, True), column_half(wide, False)
+    copies = []
+
+    def send(source, target):
+        copies.append(pltpu.make_async_copy(source, target, sems.at[len(copies)]))
+        copies[-1].start()
+
+    send(mine_c_ref, coefficients_ref.at[:, mine])
+    send(mine_u_ref, updated_ref.at[:, mine])
+    send(r_ref.at[done:, :], factor_ref.at[done:, :])
+    coefficients = jnp.concatenate(from_inverse(w_ref, terms_ref[...]), axis=0)
     c_ref[...] = coefficients
-    copies.append(pltpu.make_async_copy(c_ref, coefficients_ref, sems.at[0]))
-    copies[-1].start()
-    basis = product(panel_ref[...], inverse, 1, 1)
+    send(c_ref, coefficients_ref.at[:, other])
     tall = u_ref.shape[0] // PARTS
     for part in range(PARTS):
         at = slice(part * tall, (part + 1) * tall)
-        u_ref[at, :] = trailing_ref[at, :] - product(basis[at, :], coefficients, 1, 0)
-        copies.append(pltpu.make_async_copy(u_ref.at[at, :], updated_ref.at[at, :], sems.at[1 + part]))
-        copies[-1].start()
+        u_ref[at, :] = trailing_ref[at, other] - product(basis_ref[at, :], coefficients, 1, 0)
+        send(u_ref.at[at, :], updated_ref.at[at, other])
     for copy in copies:
         copy.wait()
 
@@ -278,36 +329,43 @@
         c = summed(c, pairs)
     blocks = width // BLOCK
     zero = [pltpu.VMEM((SUBLANES, LANES), jnp.float32)]
-    cuts = [blocks * 7 // 8, blocks]
-    state = call(functools.partial(factor_first_kernel, stop=cuts[0]), [square] * 3, g, g_other, scratch_shapes=zero)
+    cuts = [blocks * 3 // 4, blocks]
+    vmem, hbm = pl.BlockSpec(memory_space=pltpu.VMEM), pl.BlockSpec(memory_space=pl.ANY)
+    here = lambda *xs: [pltpu.with_memory_space_constraint(x, pltpu.VMEM) for x in xs]
+    inside = lambda *shapes: [pltpu.VMEM(x, jnp.float32) for x in shapes]
+    results = [jax.ShapeDtypeStruct(x, jnp.float32) for x in (square, (width, wide), (tall, wide))]
+    m, r, w, factor = pl.pallas_call(
+        functools.partial(factor_first_kernel, stop=cuts[0]),
+        out_shape=inside(square, square, square) + results[:1],
+        in_specs=[vmem] * 2,
+        out_specs=[vmem] * 3 + [hbm],
+        scratch_shapes=zero + [pltpu.SemaphoreType.DMA((cuts[0],))],
+        name="factor_first",
+        compiler_params=SMALL,
+    )(*here(g, g_other))
     c_other = sent(c, partner)
-    for i in (1,):
-        state = call(
-            functools.partial(factor_more_kernel, start=cuts[i - 1], stop=cuts[i]),
-            [square] * 3,
-            *state,
-            scratch_shapes=zero,
-            aliases={0: 0, 1: 1, 2: 2},
-        )
-    _, r, w = state
-    hbm = pl.BlockSpec(memory_space=pl.ANY)
-    return call(
-        finish_kernel,
-        [square, (width, wide), (tall, wide)],
+    _, r, w, basis, *halves = call(
+        functools.partial(factor_last_kernel, start=cuts[0], stop=cuts[1]),
+        [square] * 3 + [(tall, width), (width, wide // 2), (tall, wide // 2)],
+        m,
         r,
         w,
+        panel_block,
         c,
-        c_other,
-        panel_block,
         trailing,
-        in_vmem=False,
+        scratch_shapes=zero,
+        aliases={0: 0, 1: 1, 2: 2},
+    )
+    return pl.pallas_call(
+        functools.partial(finish_kernel, done=(cuts[0] - 1) * BLOCK),
+        out_shape=results,
+        in_specs=[vmem] * 7 + [hbm],
         out_specs=[hbm] * 3,
-        scratch_shapes=[
-            pltpu.VMEM((width, wide), jnp.float32),
-            pltpu.VMEM((tall, wide), jnp.float32),
-            pltpu.SemaphoreType.DMA((2 + PARTS,)),
-        ],
-    )
+        input_output_aliases={7: 0},
+        scratch_shapes=inside((width, wide // 2), (tall, wide // 2)) + [pltpu.SemaphoreType.DMA((4 + PARTS,))],
+        name="finish",
+        compiler_params=SMALL,
+    )(*here(r, w, basis, *halves, c_other, trailing), factor)
 
 
 def solution(mesh):

time: 47.3 us -> 46.2 us (0.977)
  Pallas kernels: 10.5 us -> 9.63 us
    pallas_call x5 -> x3, Pallas kernels: 9.37 us -> 2.62 us  [call(): pl.pallas_call(body, out_shape=shapes, input_output_aliases=aliases or {}...]
    pallas_call x0 -> x2, Pallas kernels: none -> 5.92 us  [the longest x1 4.44 us: local(): pl.pallas_call(functools.partial(factor_first_kernel, stop=cuts[0]), out_...]
  transfers between devices with their start and end apart: 11 -> 11, of which waited for: 8 -> 8; matrix products, arithmetic and copies ran while one was open for 0% -> 0% of each run, Pallas kernels for 17% -> 16%
where the time goes in v4:
time: 46.2 us; the launch traced here: 46 us
  waiting for transfers between devices  23.3 us (50%)
  starting transfers between devices  12.2 us (26%)
  Pallas kernels  9.63 us (21%)
  between operations  0.74 us (2%)
    ppermute x11, waiting for transfers between devices, sent(): return lax.ppermute(x, axis, pairs)  23.3 us
    ppermute x11, starting transfers between devices, sent(): return lax.ppermute(x, axis, pairs)  12.2 us
    pallas_call x1, Pallas kernels, local(): pl.pallas_call(functools.partial(factor_first_kernel, stop=cuts[0]), out_...  4.44 us
    pallas_call x3, Pallas kernels, call(): pl.pallas_call(body, out_shape=shapes, input_output_aliases=aliases or {}...  2.62 us
    pallas_call x1, Pallas kernels, local(): pl.pallas_call(functools.partial(finish_kernel, done=(cuts[0] - 1) * BLOC...  1.48 us
    pallas_call x1, Pallas kernels, local(): pl.pallas_call(stage_kernel, out_shape=[pltpu.VMEM(x.shape, x.dtype) for...  1.09 us
  transfers between devices with their start and end apart: 11, of which 8 were waited for; matrix products, arithmetic and copies ran while one was open for 0% of the time, Pallas kernels for 16%

profile of v4, /device:TPU:0, one launch (start us, length us, event | category | flops | bytes accessed | tf_op | source)
XLA Modules:
  0.0 46.0 jit_solution(12700146256380086605)
XLA Ops:
  0.6 3.1 %collective-permute-start = (f32[64,256]{1,0:T(8,128)}, f32[64,256]{1,0:T(8,128)S(1)}, u32[]{:S(2)}, u32[]{:S(2)}) collective-permute-start(f32[64,256]{1,0:T(8,128)} %panel_hbm.1), channel_id=1, source_target_pairs={{0,1},{1,0},{2,3},{3,2},{4,5},{5,4},{6,7},{7,6},{8,9},{9,8},{10,11... | collective-permute-start | bytes 196616 | tf_op jit(solution)/shard_map/ppermute | solution.py:299
  3.7 2.6 %collective-permute-start.1 = (f32[64,256]{1,0:T(8,128)}, f32[64,256]{1,0:T(8,128)S(1)}, u32[]{:S(2)}, u32[]{:S(2)}) collective-permute-start(f32[64,256]{1,0:T(8,128)} %panel_hbm.1), channel_id=1, source_target_pairs={{0,2},{1,3},{2,0},{3,1},{4,6},{5,7},{6,4},{7,5},{8,10},{9,11},{10,... | collective-permute-start | bytes 196616 | tf_op jit(solution)/shard_map/ppermute | solution.py:299
  6.3 0.0 collective-permute-start.2
  6.3 1.1 %stage.1 = (f32[64,256]{1,0:T(8,128)S(1)}, f32[256,512]{1,0:T(8,128)S(1)}) custom-call(f32[64,256]{1,0:T(8,128)} %panel_hbm.1, f32[256,512]{1,0:T(8,128)} %trailing_hbm.1), custom_call_target="tpu_custom_call" | custom-call | tf_op jit(solution)/shard_map/stage/pallas_call | solution.py:305
  7.5 3.8 %collective-permute-done.1.refs_2_ = f32[64,256]{1,0:T(8,128)S(1)} collective-permute-done((f32[64,256]{1,0:T(8,128)}, f32[64,256]{1,0:T(8,128)S(1)}, u32[]{:S(2)}, u32[]{:S(2)}) %collective-permute-start.1) | collective-permute-done | bytes 65568 | tf_op jit(solution)/shard_map/ppermute | solution.py:299
  11.2 1.4 %collective-permute-done.2.refs_3_ = f32[64,256]{1,0:T(8,128)S(1)} collective-permute-done((f32[64,256]{1,0:T(8,128)}, f32[64,256]{1,0:T(8,128)S(1)}, u32[]{:S(2)}, u32[]{:S(2)}) %collective-permute-start.2) | collective-permute-done | bytes 65568 | tf_op jit(solution)/shard_map/ppermute | solution.py:299
  12.6 0.3 shard_map.49
  13.0 0.4 shard_map.50
  13.4 0.1 collective-permute-start.7
  13.5 1.5 %collective-permute-done.7 = f32[256,256]{1,0:T(8,128)S(1)} collective-permute-done((f32[256,256]{1,0:T(8,128)S(1)}, f32[256,256]{1,0:T(8,128)S(1)}, u32[]{:S(2)}, u32[]{:S(2)}) %collective-permute-start.7) | collective-permute-done | bytes 262176 | tf_op jit(solution)/shard_map/ppermute | solution.py:299
  15.1 1.6 %collective-permute-start.8 = (f32[256,256]{1,0:T(8,128)S(1)}, f32[256,256]{1,0:T(8,128)S(1)}, u32[]{:S(2)}, u32[]{:S(2)}) collective-permute-start(f32[256,256]{1,0:T(8,128)S(1)} %add.21), channel_id=1, source_target_pairs={{0,8},{4,20},{8,0},{12,28},{16,24},{20,4},{24,16},{28,12},{1,9},{5... | collective-permute-start | bytes 786440 | tf_op jit(solution)/shard_map/ppermute | solution.py:299
  16.6 4.9 %collective-permute-done.8 = f32[256,256]{1,0:T(8,128)S(1)} collective-permute-done((f32[256,256]{1,0:T(8,128)S(1)}, f32[256,256]{1,0:T(8,128)S(1)}, u32[]{:S(2)}, u32[]{:S(2)}) %collective-permute-start.8) | collective-permute-done | bytes 262176 | tf_op jit(solution)/shard_map/ppermute | solution.py:299
  21.5 1.6 %collective-permute-start.9 = (f32[256,256]{1,0:T(8,128)S(1)}, f32[256,256]{1,0:T(8,128)S(1)}, u32[]{:S(2)}, u32[]{:S(2)}) collective-permute-start(f32[256,256]{1,0:T(8,128)S(1)} %add.22), channel_id=1, source_target_pairs={{0,16},{4,12},{8,24},{12,4},{16,0},{20,28},{24,8},{28,20},{1,17},{... | collective-permute-start | bytes 786440 | tf_op jit(solution)/shard_map/ppermute | solution.py:299
  23.1 4.8 %collective-permute-done.9 = f32[256,256]{1,0:T(8,128)S(1)} collective-permute-done((f32[256,256]{1,0:T(8,128)S(1)}, f32[256,256]{1,0:T(8,128)S(1)}, u32[]{:S(2)}, u32[]{:S(2)}) %collective-permute-start.9) | collective-permute-done | bytes 262176 | tf_op jit(solution)/shard_map/ppermute | solution.py:299
  28.0 0.1 collective-permute-start.10
  28.1 1.6 %collective-permute-start.4 = (f32[136,128]{1,0:T(8,128)S(1)}, f32[136,128]{1,0:T(8,128)S(1)}, u32[]{:S(2)}, u32[]{:S(2)}) collective-permute-start(f32[136,128]{1,0:T(8,128)S(1)} %add.18), channel_id=1, source_target_pairs={{0,8},{4,20},{8,0},{12,28},{16,24},{20,4},{24,16},{28,12},{1,9},{5... | collective-permute-start | bytes 208904 | tf_op jit(solution)/shard_map/ppermute | solution.py:299
  29.7 2.8 %collective-permute-done.4 = f32[136,128]{1,0:T(8,128)S(1)} collective-permute-done((f32[136,128]{1,0:T(8,128)S(1)}, f32[136,128]{1,0:T(8,128)S(1)}, u32[]{:S(2)}, u32[]{:S(2)}) %collective-permute-start.4) | collective-permute-done | bytes 69664 | tf_op jit(solution)/shard_map/ppermute | solution.py:299
  32.5 1.6 %collective-permute-start.5 = (f32[136,128]{1,0:T(8,128)S(1)}, f32[136,128]{1,0:T(8,128)S(1)}, u32[]{:S(2)}, u32[]{:S(2)}) collective-permute-start(f32[136,128]{1,0:T(8,128)S(1)} %add.19), channel_id=1, source_target_pairs={{0,16},{4,12},{8,24},{12,4},{16,0},{20,28},{24,8},{28,20},{1,17},{... | collective-permute-start | bytes 208904 | tf_op jit(solution)/shard_map/ppermute | solution.py:299
  34.1 2.8 %collective-permute-done.5 = f32[136,128]{1,0:T(8,128)S(1)} collective-permute-done((f32[136,128]{1,0:T(8,128)S(1)}, f32[136,128]{1,0:T(8,128)S(1)}, u32[]{:S(2)}, u32[]{:S(2)}) %collective-permute-start.5) | collective-permute-done | bytes 69664 | tf_op jit(solution)/shard_map/ppermute | solution.py:299
  36.9 0.1 collective-permute-start.6
  37.0 1.2 %collective-permute-done.6.other_ref = f32[136,128]{1,0:T(8,128)S(1)} collective-permute-done((f32[136,128]{1,0:T(8,128)S(1)}, f32[136,128]{1,0:T(8,128)S(1)}, u32[]{:S(2)}, u32[]{:S(2)}) %collective-permute-start.6) | collective-permute-done | bytes 69664 | tf_op jit(solution)/shard_map/ppermute | solution.py:299
  38.2 4.4 %factor_first.1 = (f32[256,256]{1,0:T(8,128)S(1)}, f32[256,256]{1,0:T(8,128)S(1)}, f32[256,256]{1,0:T(8,128)S(1)}, f32[256,256]{1,0:T(8,128)}) custom-call(f32[136,128]{1,0:T(8,128)S(1)} %add.20.mine_ref, f32[136,128]{1,0:T(8,128)S(1)} %collective-permute-done.6.other_ref), custom_call_target="tpu_custom_call" | custom-call | tf_op jit(solution)/shard_map/factor_first/pallas_call | solution.py:337
  42.7 1.9 %shard_map.51 = (f32[256,256]{1,0:T(8,128)S(1)}, f32[256,256]{1,0:T(8,128)S(1)}, f32[256,256]{1,0:T(8,128)S(1)}, f32[256,256]{1,0:T(8,128)S(1)}, f32[256,256]{1,0:T(8,128)S(1)}, /*index=5*/f32[256,256]{1,0:T(8,128)S(1)}) custom-call(f32[256,256]{1,0:T(8,128)S(1)} %get-tuple-element.22.m0_ref, ...), custom_call_target="tpu_custom_call", output_to_operand_aliasing={{0}: (0, {}), {1}: (1, {}), {2}: (2, {})} | custom-call | tf_op jit(solution)/shard_map/pallas_call | solution.py:37
  44.5 1.5 %finish.1 = (f32[256,256]{1,0:T(8,128)}, f32[256,512]{1,0:T(8,128)}, f32[256,512]{1,0:T(8,128)}) custom-call(f32[256,256]{1,0:T(8,128)S(1)} %get-tuple-element.29.refs_0_, f32[256,256]{1,0:T(8,128)S(1)} %get-tuple-element.30.refs_1_, f32[256,256]{1,0:T(8,128)S(1)} %get-tuple-element.31.refs_2_, ...), custom_call_target="tpu_custom_call", output_to_operand_aliasing={{0}: (7, {})} | custom-call | tf_op jit(solution)/shard_map/finish/pallas_call | solution.py:359
  (10 shorter events, 0.1 us)
Async XLA Ops:
  0.6 6.8 %collective-permute-start = (f32[64,256]{1,0:T(8,128)}, f32[64,256]{1,0:T(8,128)S(1)}, u32[]{:S(2)}, u32[]{:S(2)}) collective-permute-start(f32[64,256]{1,0:T(8,128)} %panel_hbm.1), channel_id=1, source_target_pairs={{0,1},{1,0},{2,3},{3,2},{4,5},{5,4},{6,7},{7,6},{8,9},{9,8},{10,11... | collective-permute-start | bytes 196616 | tf_op jit(solution)/shard_map/ppermute | solution.py:299
  3.7 7.5 %collective-permute-start.1 = (f32[64,256]{1,0:T(8,128)}, f32[64,256]{1,0:T(8,128)S(1)}, u32[]{:S(2)}, u32[]{:S(2)}) collective-permute-start(f32[64,256]{1,0:T(8,128)} %panel_hbm.1), channel_id=1, source_target_pairs={{0,2},{1,3},{2,0},{3,1},{4,6},{5,7},{6,4},{7,5},{8,10},{9,11},{10,... | collective-permute-start | bytes 196616 | tf_op jit(solution)/shard_map/ppermute | solution.py:299
  6.3 6.3 %collective-permute-start.2 = (f32[64,256]{1,0:T(8,128)}, f32[64,256]{1,0:T(8,128)S(1)}, u32[]{:S(2)}, u32[]{:S(2)}) collective-permute-start(f32[64,256]{1,0:T(8,128)} %panel_hbm.1), channel_id=1, source_target_pairs={{0,3},{1,2},{2,1},{3,0},{4,7},{5,6},{6,5},{7,4},{8,11},{9,10},{10,... | collective-permute-start | bytes 196616 | tf_op jit(solution)/shard_map/ppermute | solution.py:299
  13.4 1.6 %collective-permute-start.7 = (f32[256,256]{1,0:T(8,128)S(1)}, f32[256,256]{1,0:T(8,128)S(1)}, u32[]{:S(2)}, u32[]{:S(2)}) collective-permute-start(f32[256,256]{1,0:T(8,128)S(1)} %get-tuple-element.28), channel_id=1, source_target_pairs={{0,4},{4,0},{8,12},{12,8},{16,20},{20,16},{24,28},{28,24},{1,5},{5... | collective-permute-start | bytes 786440 | tf_op jit(solution)/shard_map/ppermute | solution.py:299
  15.1 6.4 %collective-permute-start.8 = (f32[256,256]{1,0:T(8,128)S(1)}, f32[256,256]{1,0:T(8,128)S(1)}, u32[]{:S(2)}, u32[]{:S(2)}) collective-permute-start(f32[256,256]{1,0:T(8,128)S(1)} %add.21), channel_id=1, source_target_pairs={{0,8},{4,20},{8,0},{12,28},{16,24},{20,4},{24,16},{28,12},{1,9},{5... | collective-permute-start | bytes 786440 | tf_op jit(solution)/shard_map/ppermute | solution.py:299
  21.5 6.4 %collective-permute-start.9 = (f32[256,256]{1,0:T(8,128)S(1)}, f32[256,256]{1,0:T(8,128)S(1)}, u32[]{:S(2)}, u32[]{:S(2)}) collective-permute-start(f32[256,256]{1,0:T(8,128)S(1)} %add.22), channel_id=1, source_target_pairs={{0,16},{4,12},{8,24},{12,4},{16,0},{20,28},{24,8},{28,20},{1,17},{... | collective-permute-start | bytes 786440 | tf_op jit(solution)/shard_map/ppermute | solution.py:299
  23.1 5.0 %collective-permute-start.3 = (f32[136,128]{1,0:T(8,128)S(1)}, f32[136,128]{1,0:T(8,128)S(1)}, u32[]{:S(2)}, u32[]{:S(2)}) collective-permute-start(f32[136,128]{1,0:T(8,128)S(1)} %get-tuple-element.21), channel_id=1, source_target_pairs={{0,4},{4,0},{8,12},{12,8},{16,20},{20,16},{24,28},{28,24},{1,5},{5... | collective-permute-start | bytes 208904 | tf_op jit(solution)/shard_map/ppermute | solution.py:299
  28.0 16.5 %collective-permute-start.10 = (f32[256,256]{1,0:T(8,128)S(1)}, f32[256,256]{1,0:T(8,128)S(1)}, u32[]{:S(2)}, u32[]{:S(2)}) collective-permute-start(f32[256,256]{1,0:T(8,128)S(1)} %add.23.terms_ref), channel_id=1, source_target_pairs={{0,4},{4,0},{8,12},{12,8},{16,20},{20,16},{24,28},{28,24},{1,5},{5... | collective-permute-start | bytes 786440 | tf_op jit(solution)/shard_map/ppermute | solution.py:299
  28.1 4.4 %collective-permute-start.4 = (f32[136,128]{1,0:T(8,128)S(1)}, f32[136,128]{1,0:T(8,128)S(1)}, u32[]{:S(2)}, u32[]{:S(2)}) collective-permute-start(f32[136,128]{1,0:T(8,128)S(1)} %add.18), channel_id=1, source_target_pairs={{0,8},{4,20},{8,0},{12,28},{16,24},{20,4},{24,16},{28,12},{1,9},{5... | collective-permute-start | bytes 208904 | tf_op jit(solution)/shard_map/ppermute | solution.py:299
  32.5 4.4 %collective-permute-start.5 = (f32[136,128]{1,0:T(8,128)S(1)}, f32[136,128]{1,0:T(8,128)S(1)}, u32[]{:S(2)}, u32[]{:S(2)}) collective-permute-start(f32[136,128]{1,0:T(8,128)S(1)} %add.19), channel_id=1, source_target_pairs={{0,16},{4,12},{8,24},{12,4},{16,0},{20,28},{24,8},{28,20},{1,17},{... | collective-permute-start | bytes 208904 | tf_op jit(solution)/shard_map/ppermute | solution.py:299
  36.9 1.3 %collective-permute-start.6 = (f32[136,128]{1,0:T(8,128)S(1)}, f32[136,128]{1,0:T(8,128)S(1)}, u32[]{:S(2)}, u32[]{:S(2)}) collective-permute-start(f32[136,128]{1,0:T(8,128)S(1)} %add.20.mine_ref), channel_id=1, source_target_pairs={{0,4},{4,0},{8,12},{12,8},{16,20},{20,16},{24,28},{28,24},{1,5},{5... | collective-permute-start | bytes 208904 | tf_op jit(solution)/shard_map/ppermute | solution.py:299

commit v5 on v4

--- a/solution.py
+++ b/solution.py
@@ -8,7 +8,7 @@
 from jax.sharding import PartitionSpec as P
 
 
-LANES, SUBLANES, BLOCK, INNER, PARTS = 128, 8, 32, 4, 4
+LANES, SUBLANES, BLOCK, INNER, PARTS = 128, 8, 32, 4, 1
 
 SMALL = pltpu.CompilerParams(vmem_limit_bytes=16 << 20)
 
@@ -198,7 +198,9 @@
         m_ref[below:, :] = jnp.where((c >= base) & (c < below), 0.0, old) - change
 
 
-def factor_first_kernel(mine_ref, other_ref, m_ref, r_ref, w_ref, factor_ref, zero_ref, sem, *, stop):
+def factor_first_kernel(
+    mine_ref, other_ref, panel_ref, m_ref, r_ref, w_ref, basis_ref, factor_ref, zero_ref, sem, *, stop
+):
     zero_ref[...] = jnp.zeros_like(zero_ref)
     unpack(mine_ref, other_ref, m_ref)
     copies = []
@@ -208,6 +210,8 @@
             at = slice(k * BLOCK, (k + 1) * BLOCK)
             copies.append(pltpu.make_async_copy(r_ref.at[at, :], factor_ref.at[at, :], sem.at[k]))
             copies[-1].start()
+    half = w_ref.shape[0] // 2
+    basis_ref[...] = product(panel_ref[:, :half], w_ref[:half, :half], 1, 1)
     for copy in copies:
         copy.wait()
 
@@ -223,13 +227,13 @@
 
 
 def factor_last_kernel(
-    m0_ref, r0_ref, w0_ref, panel_ref, terms_ref, trailing_ref, m_ref, r_ref, w_ref, basis_ref, c_ref, u_ref, zero_ref, *, start, stop
+    m0_ref, r0_ref, w0_ref, basis0_ref, panel_ref, terms_ref, trailing_ref, m_ref, r_ref, w_ref, basis_ref, c_ref, u_ref, zero_ref, *, start, stop
 ):
     zero_ref[...] = jnp.zeros_like(zero_ref)
     for k in range(start, stop):
         factor_block(m_ref, r_ref, w_ref, zero_ref, k)
     half = w_ref.shape[0] // 2
-    basis_ref[:, :half] = product(panel_ref[:, :half], w_ref[:half, :half], 1, 1)
+    basis_ref[:, :half] = basis0_ref[...]
     basis_ref[:, half:] = product(panel_ref[...], w_ref[half:, :], 1, 1)
     coefficients = jnp.concatenate(from_inverse(w_ref, terms_ref[...]), axis=0)
     c_ref[...] = coefficients
@@ -334,15 +338,15 @@
     here = lambda *xs: [pltpu.with_memory_space_constraint(x, pltpu.VMEM) for x in xs]
     inside = lambda *shapes: [pltpu.VMEM(x, jnp.float32) for x in shapes]
     results = [jax.ShapeDtypeStruct(x, jnp.float32) for x in (square, (width, wide), (tall, wide))]
-    m, r, w, factor = pl.pallas_call(
+    m, r, w, basis, factor = pl.pallas_call(
         functools.partial(factor_first_kernel, stop=cuts[0]),
-        out_shape=inside(square, square, square) + results[:1],
-        in_specs=[vmem] * 2,
-        out_specs=[vmem] * 3 + [hbm],
+        out_shape=inside(square, square, square, (tall, half)) + results[:1],
+        in_specs=[vmem] * 3,
+        out_specs=[vmem] * 4 + [hbm],
         scratch_shapes=zero + [pltpu.SemaphoreType.DMA((cuts[0],))],
         name="factor_first",
         compiler_params=SMALL,
-    )(*here(g, g_other))
+    )(*here(g, g_other, panel_block))
     c_other = sent(c, partner)
     _, r, w, basis, *halves = call(
         functools.partial(factor_last_kernel, start=cuts[0], stop=cuts[1]),
@@ -350,6 +354,7 @@
         m,
         r,
         w,
+        basis,
         panel_block,
         c,
         trailing,

time: 46.2 us -> 46 us (level)
  no operation moved by 1% of the time
where the time goes in v5:
time: 46 us; the launch traced here: 45.9 us
  waiting for transfers between devices  23.3 us (51%)
  starting transfers between devices  12.2 us (27%)
  Pallas kernels  9.5 us (21%)
  between operations  0.75 us (2%)
    ppermute x11, waiting for transfers between devices, sent(): return lax.ppermute(x, axis, pairs)  23.3 us
    ppermute x11, starting transfers between devices, sent(): return lax.ppermute(x, axis, pairs)  12.2 us
    pallas_call x1, Pallas kernels, local(): pl.pallas_call(functools.partial(factor_first_kernel, stop=cuts[0]), out_...  4.48 us
    pallas_call x3, Pallas kernels, call(): pl.pallas_call(body, out_shape=shapes, input_output_aliases=aliases or {}...  2.51 us
    pallas_call x1, Pallas kernels, local(): pl.pallas_call(functools.partial(finish_kernel, done=(cuts[0] - 1) * BLOC...  1.42 us
    pallas_call x1, Pallas kernels, local(): pl.pallas_call(stage_kernel, out_shape=[pltpu.VMEM(x.shape, x.dtype) for...  1.09 us
  transfers between devices with their start and end apart: 11, of which 8 were waited for; matrix products, arithmetic and copies ran while one was open for 0% of the time, Pallas kernels for 16%

profile of v5, /device:TPU:0, one launch (start us, length us, event | category | flops | bytes accessed | tf_op | source)
XLA Modules:
  0.0 45.9 jit_solution(10740531807238339305)
XLA Ops:
  0.6 3.1 %collective-permute-start = (f32[64,256]{1,0:T(8,128)}, f32[64,256]{1,0:T(8,128)S(1)}, u32[]{:S(2)}, u32[]{:S(2)}) collective-permute-start(f32[64,256]{1,0:T(8,128)} %panel_hbm.1), channel_id=1, source_target_pairs={{0,1},{1,0},{2,3},{3,2},{4,5},{5,4},{6,7},{7,6},{8,9},{9,8},{10,11... | collective-permute-start | bytes 196616 | tf_op jit(solution)/shard_map/ppermute | solution.py:303
  3.7 2.6 %collective-permute-start.1 = (f32[64,256]{1,0:T(8,128)}, f32[64,256]{1,0:T(8,128)S(1)}, u32[]{:S(2)}, u32[]{:S(2)}) collective-permute-start(f32[64,256]{1,0:T(8,128)} %panel_hbm.1), channel_id=1, source_target_pairs={{0,2},{1,3},{2,0},{3,1},{4,6},{5,7},{6,4},{7,5},{8,10},{9,11},{10,... | collective-permute-start | bytes 196616 | tf_op jit(solution)/shard_map/ppermute | solution.py:303
  6.3 0.0 collective-permute-start.2
  6.3 1.1 %stage.1 = (f32[64,256]{1,0:T(8,128)S(1)}, f32[256,512]{1,0:T(8,128)S(1)}) custom-call(f32[64,256]{1,0:T(8,128)} %panel_hbm.1, f32[256,512]{1,0:T(8,128)} %trailing_hbm.1), custom_call_target="tpu_custom_call" | custom-call | tf_op jit(solution)/shard_map/stage/pallas_call | solution.py:309
  7.5 3.8 %collective-permute-done.1.refs_2_ = f32[64,256]{1,0:T(8,128)S(1)} collective-permute-done((f32[64,256]{1,0:T(8,128)}, f32[64,256]{1,0:T(8,128)S(1)}, u32[]{:S(2)}, u32[]{:S(2)}) %collective-permute-start.1) | collective-permute-done | bytes 65568 | tf_op jit(solution)/shard_map/ppermute | solution.py:303
  11.2 1.4 %collective-permute-done.2.refs_3_ = f32[64,256]{1,0:T(8,128)S(1)} collective-permute-done((f32[64,256]{1,0:T(8,128)}, f32[64,256]{1,0:T(8,128)S(1)}, u32[]{:S(2)}, u32[]{:S(2)}) %collective-permute-start.2) | collective-permute-done | bytes 65568 | tf_op jit(solution)/shard_map/ppermute | solution.py:303
  12.6 0.3 shard_map.49
  13.0 0.4 shard_map.50
  13.4 0.1 collective-permute-start.7
  13.5 1.5 %collective-permute-done.7 = f32[256,256]{1,0:T(8,128)S(1)} collective-permute-done((f32[256,256]{1,0:T(8,128)S(1)}, f32[256,256]{1,0:T(8,128)S(1)}, u32[]{:S(2)}, u32[]{:S(2)}) %collective-permute-start.7) | collective-permute-done | bytes 262176 | tf_op jit(solution)/shard_map/ppermute | solution.py:303
  15.1 1.6 %collective-permute-start.8 = (f32[256,256]{1,0:T(8,128)S(1)}, f32[256,256]{1,0:T(8,128)S(1)}, u32[]{:S(2)}, u32[]{:S(2)}) collective-permute-start(f32[256,256]{1,0:T(8,128)S(1)} %add.21), channel_id=1, source_target_pairs={{0,8},{4,20},{8,0},{12,28},{16,24},{20,4},{24,16},{28,12},{1,9},{5... | collective-permute-start | bytes 786440 | tf_op jit(solution)/shard_map/ppermute | solution.py:303
  16.6 4.9 %collective-permute-done.8 = f32[256,256]{1,0:T(8,128)S(1)} collective-permute-done((f32[256,256]{1,0:T(8,128)S(1)}, f32[256,256]{1,0:T(8,128)S(1)}, u32[]{:S(2)}, u32[]{:S(2)}) %collective-permute-start.8) | collective-permute-done | bytes 262176 | tf_op jit(solution)/shard_map/ppermute | solution.py:303
  21.5 1.6 %collective-permute-start.9 = (f32[256,256]{1,0:T(8,128)S(1)}, f32[256,256]{1,0:T(8,128)S(1)}, u32[]{:S(2)}, u32[]{:S(2)}) collective-permute-start(f32[256,256]{1,0:T(8,128)S(1)} %add.22), channel_id=1, source_target_pairs={{0,16},{4,12},{8,24},{12,4},{16,0},{20,28},{24,8},{28,20},{1,17},{... | collective-permute-start | bytes 786440 | tf_op jit(solution)/shard_map/ppermute | solution.py:303
  23.1 4.8 %collective-permute-done.9 = f32[256,256]{1,0:T(8,128)S(1)} collective-permute-done((f32[256,256]{1,0:T(8,128)S(1)}, f32[256,256]{1,0:T(8,128)S(1)}, u32[]{:S(2)}, u32[]{:S(2)}) %collective-permute-start.9) | collective-permute-done | bytes 262176 | tf_op jit(solution)/shard_map/ppermute | solution.py:303
  28.0 0.1 collective-permute-start.10
  28.1 1.6 %collective-permute-start.4 = (f32[136,128]{1,0:T(8,128)S(1)}, f32[136,128]{1,0:T(8,128)S(1)}, u32[]{:S(2)}, u32[]{:S(2)}) collective-permute-start(f32[136,128]{1,0:T(8,128)S(1)} %add.18), channel_id=1, source_target_pairs={{0,8},{4,20},{8,0},{12,28},{16,24},{20,4},{24,16},{28,12},{1,9},{5... | collective-permute-start | bytes 208904 | tf_op jit(solution)/shard_map/ppermute | solution.py:303
  29.7 2.8 %collective-permute-done.4 = f32[136,128]{1,0:T(8,128)S(1)} collective-permute-done((f32[136,128]{1,0:T(8,128)S(1)}, f32[136,128]{1,0:T(8,128)S(1)}, u32[]{:S(2)}, u32[]{:S(2)}) %collective-permute-start.4) | collective-permute-done | bytes 69664 | tf_op jit(solution)/shard_map/ppermute | solution.py:303
  32.5 1.6 %collective-permute-start.5 = (f32[136,128]{1,0:T(8,128)S(1)}, f32[136,128]{1,0:T(8,128)S(1)}, u32[]{:S(2)}, u32[]{:S(2)}) collective-permute-start(f32[136,128]{1,0:T(8,128)S(1)} %add.19), channel_id=1, source_target_pairs={{0,16},{4,12},{8,24},{12,4},{16,0},{20,28},{24,8},{28,20},{1,17},{... | collective-permute-start | bytes 208904 | tf_op jit(solution)/shard_map/ppermute | solution.py:303
  34.1 2.8 %collective-permute-done.5 = f32[136,128]{1,0:T(8,128)S(1)} collective-permute-done((f32[136,128]{1,0:T(8,128)S(1)}, f32[136,128]{1,0:T(8,128)S(1)}, u32[]{:S(2)}, u32[]{:S(2)}) %collective-permute-start.5) | collective-permute-done | bytes 69664 | tf_op jit(solution)/shard_map/ppermute | solution.py:303
  36.9 0.1 collective-permute-start.6
  37.0 1.2 %collective-permute-done.6.other_ref = f32[136,128]{1,0:T(8,128)S(1)} collective-permute-done((f32[136,128]{1,0:T(8,128)S(1)}, f32[136,128]{1,0:T(8,128)S(1)}, u32[]{:S(2)}, u32[]{:S(2)}) %collective-permute-start.6) | collective-permute-done | bytes 69664 | tf_op jit(solution)/shard_map/ppermute | solution.py:303
  38.2 4.5 %factor_first.1 = (f32[256,256]{1,0:T(8,128)S(1)}, f32[256,256]{1,0:T(8,128)S(1)}, f32[256,256]{1,0:T(8,128)S(1)}, f32[256,128]{1,0:T(8,128)S(1)}, f32[256,256]{1,0:T(8,128)}) custom-call(f32[136,128]{1,0:T(8,128)S(1)} %add.20.mine_ref, f32[136,128]{1,0:T(8,128)S(1)} %collective-permute-done.6.other_ref, f32[256,256]{1,0:T(8,128)S(1)} %get-tuple-element.23.panel_ref), custom_call_target="tpu_custom_call" | custom-call | tf_op jit(solution)/shard_map/factor_first/pallas_call | solution.py:341
  42.7 1.7 %shard_map.51 = (f32[256,256]{1,0:T(8,128)S(1)}, f32[256,256]{1,0:T(8,128)S(1)}, f32[256,256]{1,0:T(8,128)S(1)}, f32[256,256]{1,0:T(8,128)S(1)}, f32[256,256]{1,0:T(8,128)S(1)}, /*index=5*/f32[256,256]{1,0:T(8,128)S(1)}) custom-call(f32[256,256]{1,0:T(8,128)S(1)} %get-tuple-element.24.m0_ref, ...), custom_call_target="tpu_custom_call", output_to_operand_aliasing={{0}: (0, {}), {1}: (1, {}), {2}: (2, {})} | custom-call | tf_op jit(solution)/shard_map/pallas_call | solution.py:37
  44.5 1.4 %finish.1 = (f32[256,256]{1,0:T(8,128)}, f32[256,512]{1,0:T(8,128)}, f32[256,512]{1,0:T(8,128)}) custom-call(f32[256,256]{1,0:T(8,128)S(1)} %get-tuple-element.31.refs_0_, f32[256,256]{1,0:T(8,128)S(1)} %get-tuple-element.32.refs_1_, f32[256,256]{1,0:T(8,128)S(1)} %get-tuple-element.33.refs_2_, ...), custom_call_target="tpu_custom_call", output_to_operand_aliasing={{0}: (7, {})} | custom-call | tf_op jit(solution)/shard_map/finish/pallas_call | solution.py:364
  (10 shorter events, 0.1 us)
Async XLA Ops:
  0.6 6.8 %collective-permute-start = (f32[64,256]{1,0:T(8,128)}, f32[64,256]{1,0:T(8,128)S(1)}, u32[]{:S(2)}, u32[]{:S(2)}) collective-permute-start(f32[64,256]{1,0:T(8,128)} %panel_hbm.1), channel_id=1, source_target_pairs={{0,1},{1,0},{2,3},{3,2},{4,5},{5,4},{6,7},{7,6},{8,9},{9,8},{10,11... | collective-permute-start | bytes 196616 | tf_op jit(solution)/shard_map/ppermute | solution.py:303
  3.7 7.5 %collective-permute-start.1 = (f32[64,256]{1,0:T(8,128)}, f32[64,256]{1,0:T(8,128)S(1)}, u32[]{:S(2)}, u32[]{:S(2)}) collective-permute-start(f32[64,256]{1,0:T(8,128)} %panel_hbm.1), channel_id=1, source_target_pairs={{0,2},{1,3},{2,0},{3,1},{4,6},{5,7},{6,4},{7,5},{8,10},{9,11},{10,... | collective-permute-start | bytes 196616 | tf_op jit(solution)/shard_map/ppermute | solution.py:303
  6.3 6.3 %collective-permute-start.2 = (f32[64,256]{1,0:T(8,128)}, f32[64,256]{1,0:T(8,128)S(1)}, u32[]{:S(2)}, u32[]{:S(2)}) collective-permute-start(f32[64,256]{1,0:T(8,128)} %panel_hbm.1), channel_id=1, source_target_pairs={{0,3},{1,2},{2,1},{3,0},{4,7},{5,6},{6,5},{7,4},{8,11},{9,10},{10,... | collective-permute-start | bytes 196616 | tf_op jit(solution)/shard_map/ppermute | solution.py:303
  13.4 1.6 %collective-permute-start.7 = (f32[256,256]{1,0:T(8,128)S(1)}, f32[256,256]{1,0:T(8,128)S(1)}, u32[]{:S(2)}, u32[]{:S(2)}) collective-permute-start(f32[256,256]{1,0:T(8,128)S(1)} %get-tuple-element.30), channel_id=1, source_target_pairs={{0,4},{4,0},{8,12},{12,8},{16,20},{20,16},{24,28},{28,24},{1,5},{5... | collective-permute-start | bytes 786440 | tf_op jit(solution)/shard_map/ppermute | solution.py:303
  15.1 6.4 %collective-permute-start.8 = (f32[256,256]{1,0:T(8,128)S(1)}, f32[256,256]{1,0:T(8,128)S(1)}, u32[]{:S(2)}, u32[]{:S(2)}) collective-permute-start(f32[256,256]{1,0:T(8,128)S(1)} %add.21), channel_id=1, source_target_pairs={{0,8},{4,20},{8,0},{12,28},{16,24},{20,4},{24,16},{28,12},{1,9},{5... | collective-permute-start | bytes 786440 | tf_op jit(solution)/shard_map/ppermute | solution.py:303
  21.5 6.4 %collective-permute-start.9 = (f32[256,256]{1,0:T(8,128)S(1)}, f32[256,256]{1,0:T(8,128)S(1)}, u32[]{:S(2)}, u32[]{:S(2)}) collective-permute-start(f32[256,256]{1,0:T(8,128)S(1)} %add.22), channel_id=1, source_target_pairs={{0,16},{4,12},{8,24},{12,4},{16,0},{20,28},{24,8},{28,20},{1,17},{... | collective-permute-start | bytes 786440 | tf_op jit(solution)/shard_map/ppermute | solution.py:303
  23.1 5.0 %collective-permute-start.3 = (f32[136,128]{1,0:T(8,128)S(1)}, f32[136,128]{1,0:T(8,128)S(1)}, u32[]{:S(2)}, u32[]{:S(2)}) collective-permute-start(f32[136,128]{1,0:T(8,128)S(1)} %get-tuple-element.22), channel_id=1, source_target_pairs={{0,4},{4,0},{8,12},{12,8},{16,20},{20,16},{24,28},{28,24},{1,5},{5... | collective-permute-start | bytes 208904 | tf_op jit(solution)/shard_map/ppermute | solution.py:303
  28.0 16.5 %collective-permute-start.10 = (f32[256,256]{1,0:T(8,128)S(1)}, f32[256,256]{1,0:T(8,128)S(1)}, u32[]{:S(2)}, u32[]{:S(2)}) collective-permute-start(f32[256,256]{1,0:T(8,128)S(1)} %add.23.terms_ref), channel_id=1, source_target_pairs={{0,4},{4,0},{8,12},{12,8},{16,20},{20,16},{24,28},{28,24},{1,5},{5... | collective-permute-start | bytes 786440 | tf_op jit(solution)/shard_map/ppermute | solution.py:303
  28.1 4.4 %collective-permute-start.4 = (f32[136,128]{1,0:T(8,128)S(1)}, f32[136,128]{1,0:T(8,128)S(1)}, u32[]{:S(2)}, u32[]{:S(2)}) collective-permute-start(f32[136,128]{1,0:T(8,128)S(1)} %add.18), channel_id=1, source_target_pairs={{0,8},{4,20},{8,0},{12,28},{16,24},{20,4},{24,16},{28,12},{1,9},{5... | collective-permute-start | bytes 208904 | tf_op jit(solution)/shard_map/ppermute | solution.py:303
  32.5 4.4 %collective-permute-start.5 = (f32[136,128]{1,0:T(8,128)S(1)}, f32[136,128]{1,0:T(8,128)S(1)}, u32[]{:S(2)}, u32[]{:S(2)}) collective-permute-start(f32[136,128]{1,0:T(8,128)S(1)} %add.19), channel_id=1, source_target_pairs={{0,16},{4,12},{8,24},{12,4},{16,0},{20,28},{24,8},{28,20},{1,17},{... | collective-permute-start | bytes 208904 | tf_op jit(solution)/shard_map/ppermute | solution.py:303
  36.9 1.3 %collective-permute-start.6 = (f32[136,128]{1,0:T(8,128)S(1)}, f32[136,128]{1,0:T(8,128)S(1)}, u32[]{:S(2)}, u32[]{:S(2)}) collective-permute-start(f32[136,128]{1,0:T(8,128)S(1)} %add.20.mine_ref), channel_id=1, source_target_pairs={{0,4},{4,0},{8,12},{12,8},{16,20},{20,16},{24,28},{28,24},{1,5},{5... | collective-permute-start | bytes 208904 | tf_op jit(solution)/shard_map/ppermute | solution.py:303

commit v6 on v5

--- a/solution.py
+++ b/solution.py
@@ -29,9 +29,9 @@
     )
 
 
-def call(body, outs, *args, aliases=None, in_vmem=True, **extra):
+def call(body, outs, *args, aliases=None, **extra):
     block = pl.BlockSpec(memory_space=pltpu.VMEM)
-    shapes = [(pltpu.VMEM if in_vmem else jax.ShapeDtypeStruct)(s, jnp.float32) for s in outs]
+    shapes = [pltpu.VMEM(s, jnp.float32) if isinstance(s, tuple) else s for s in outs]
     args = [pltpu.with_memory_space_constraint(x, pltpu.VMEM) for x in args]
     extra = {"in_specs": [block] * len(args), "out_specs": [block] * len(outs), "compiler_params": SMALL} | extra
     return pl.pallas_call(body, out_shape=shapes, input_output_aliases=aliases or {}, **extra)(*args)
@@ -216,9 +216,18 @@
         copy.wait()
 
 
-def from_inverse(w_ref, x):
-    half = w_ref.shape[0] // 2
-    return product(w_ref[:half, :half], x[:half, :], 1, 0), product(w_ref[half:, :], x, 1, 0)
+def stack(x):
+    high, low = split(x)
+    return jnp.concatenate([high, high, low], axis=1)
+
+
+def stacked_product(stacked, right):
+    high, low = split(right)
+    return jnp.dot(stacked, jnp.concatenate([high, low, high], axis=0), preferred_element_type=jnp.float32)
+
+
+def from_inverse(top, low, x):
+    return stacked_product(top, x[: x.shape[0] // 2, :]), stacked_product(low, x)
 
 
 def column_half(half, mine):
@@ -227,18 +236,20 @@
 
 
 def factor_last_kernel(
-    m0_ref, r0_ref, w0_ref, basis0_ref, panel_ref, terms_ref, trailing_ref, m_ref, r_ref, w_ref, basis_ref, c_ref, u_ref, zero_ref, *, start, stop
+    m0_ref, r0_ref, w0_ref, basis0_ref, panel_ref, terms_ref, trailing_ref, m_ref, r_ref, w_ref, top_ref, low_ref, basis_ref, c_ref, u_ref, zero_ref, *, start, stop
 ):
     zero_ref[...] = jnp.zeros_like(zero_ref)
     for k in range(start, stop):
         factor_block(m_ref, r_ref, w_ref, zero_ref, k)
     half = w_ref.shape[0] // 2
-    basis_ref[:, :half] = basis0_ref[...]
-    basis_ref[:, half:] = product(panel_ref[...], w_ref[half:, :], 1, 1)
-    coefficients = jnp.concatenate(from_inverse(w_ref, terms_ref[...]), axis=0)
+    rest = product(panel_ref[...], w_ref[half:, :], 1, 1)
+    basis_ref[...] = stack(jnp.concatenate([basis0_ref[...], rest], axis=1))
+    top_ref[...] = stack(w_ref[:half, :half])
+    low_ref[...] = stack(w_ref[half:, :])
+    coefficients = jnp.concatenate(from_inverse(top_ref[...], low_ref[...], terms_ref[...]), axis=0)
     c_ref[...] = coefficients
     columns = column_half(c_ref.shape[1], True)
-    u_ref[...] = trailing_ref[:, columns] - product(basis_ref[...], coefficients, 1, 0)
+    u_ref[...] = trailing_ref[:, columns] - stacked_product(basis_ref[...], coefficients)
 
 
 def cross_kernel(panel_ref, trailing_ref, keep_ref, send_ref):
@@ -258,7 +269,7 @@
 
 
 def finish_kernel(*refs, done):
-    r_ref, w_ref, basis_ref, mine_c_ref, mine_u_ref, terms_ref, trailing_ref, _, *outs, c_ref, u_ref, sems = refs
+    r_ref, top_ref, low_ref, basis_ref, mine_c_ref, mine_u_ref, terms_ref, trailing_ref, _, *outs, c_ref, u_ref, sems = refs
     factor_ref, coefficients_ref, updated_ref = outs
     _, wide = c_ref.shape
     mine, other = column_half(wide, True), column_half(wide, False)
@@ -271,13 +282,13 @@
     send(mine_c_ref, coefficients_ref.at[:, mine])
     send(mine_u_ref, updated_ref.at[:, mine])
     send(r_ref.at[done:, :], factor_ref.at[done:, :])
-    coefficients = jnp.concatenate(from_inverse(w_ref, terms_ref[...]), axis=0)
+    coefficients = jnp.concatenate(from_inverse(top_ref[...], low_ref[...], terms_ref[...]), axis=0)
     c_ref[...] = coefficients
     send(c_ref, coefficients_ref.at[:, other])
     tall = u_ref.shape[0] // PARTS
     for part in range(PARTS):
         at = slice(part * tall, (part + 1) * tall)
-        u_ref[at, :] = trailing_ref[at, other] - product(basis_ref[at, :], coefficients, 1, 0)
+        u_ref[at, :] = trailing_ref[at, other] - stacked_product(basis_ref[at, :], coefficients)
         send(u_ref.at[at, :], updated_ref.at[at, other])
     for copy in copies:
         copy.wait()
@@ -333,7 +344,7 @@
         c = summed(c, pairs)
     blocks = width // BLOCK
     zero = [pltpu.VMEM((SUBLANES, LANES), jnp.float32)]
-    cuts = [blocks * 3 // 4, blocks]
+    cuts = [blocks * 7 // 8, blocks]
     vmem, hbm = pl.BlockSpec(memory_space=pltpu.VMEM), pl.BlockSpec(memory_space=pl.ANY)
     here = lambda *xs: [pltpu.with_memory_space_constraint(x, pltpu.VMEM) for x in xs]
     inside = lambda *shapes: [pltpu.VMEM(x, jnp.float32) for x in shapes]
@@ -348,9 +359,10 @@
         compiler_params=SMALL,
     )(*here(g, g_other, panel_block))
     c_other = sent(c, partner)
-    _, r, w, basis, *halves = call(
+    stacks = [pltpu.VMEM(x, jnp.bfloat16) for x in ((half, 3 * half), (half, 3 * width), (tall, 3 * width))]
+    _, r, _, top, low, basis, *halves = call(
         functools.partial(factor_last_kernel, start=cuts[0], stop=cuts[1]),
-        [square] * 3 + [(tall, width), (width, wide // 2), (tall, wide // 2)],
+        [square] * 3 + stacks + [(width, wide // 2), (tall, wide // 2)],
         m,
         r,
         w,
@@ -364,13 +376,13 @@
     return pl.pallas_call(
         functools.partial(finish_kernel, done=(cuts[0] - 1) * BLOCK),
         out_shape=results,
-        in_specs=[vmem] * 7 + [hbm],
+        in_specs=[vmem] * 8 + [hbm],
         out_specs=[hbm] * 3,
-        input_output_aliases={7: 0},
+        input_output_aliases={8: 0},
         scratch_shapes=inside((width, wide // 2), (tall, wide // 2)) + [pltpu.SemaphoreType.DMA((4 + PARTS,))],
         name="finish",
         compiler_params=SMALL,
-    )(*here(r, w, basis, *halves, c_other, trailing), factor)
+    )(*here(r, top, low, basis, *halves, c_other, trailing), factor)
 
 
 def solution(mesh):

time: 46 us -> 46.1 us (level)
    pallas_call x1, Pallas kernels: 4.48 us -> 5.23 us  [local(): pl.pallas_call(functools.partial(factor_first_kernel, stop=cuts[0]), out_...]
    pallas_call x3, Pallas kernels: 2.51 us -> 1.83 us  [call(): pl.pallas_call(body, out_shape=shapes, input_output_aliases=aliases or {}...]
where the time goes in v6:
time: 46.1 us; the launch traced here: 45.9 us
  waiting for transfers between devices  23.3 us (51%)
  starting transfers between devices  12.2 us (26%)
  Pallas kernels  9.55 us (21%)
  between operations  0.75 us (2%)
    ppermute x11, waiting for transfers between devices, sent(): return lax.ppermute(x, axis, pairs)  23.3 us
    ppermute x11, starting transfers between devices, sent(): return lax.ppermute(x, axis, pairs)  12.2 us
    pallas_call x1, Pallas kernels, local(): pl.pallas_call(functools.partial(factor_first_kernel, stop=cuts[0]), out_...  5.23 us
    pallas_call x3, Pallas kernels, call(): pl.pallas_call(body, out_shape=shapes, input_output_aliases=aliases or {}...  1.83 us
    pallas_call x1, Pallas kernels, local(): pl.pallas_call(functools.partial(finish_kernel, done=(cuts[0] - 1) * BLOC...  1.4 us
    pallas_call x1, Pallas kernels, local(): pl.pallas_call(stage_kernel, out_shape=[pltpu.VMEM(x.shape, x.dtype) for...  1.09 us
  transfers between devices with their start and end apart: 11, of which 8 were waited for; matrix products, arithmetic and copies ran while one was open for 0% of the time, Pallas kernels for 16%

profile of v6, /device:TPU:0, one launch (start us, length us, event | category | flops | bytes accessed | tf_op | source)
XLA Modules:
  0.0 45.9 jit_solution(3927418721513595268)
XLA Ops:
  0.6 3.1 %collective-permute-start = (f32[64,256]{1,0:T(8,128)}, f32[64,256]{1,0:T(8,128)S(1)}, u32[]{:S(2)}, u32[]{:S(2)}) collective-permute-start(f32[64,256]{1,0:T(8,128)} %panel_hbm.1), channel_id=1, source_target_pairs={{0,1},{1,0},{2,3},{3,2},{4,5},{5,4},{6,7},{7,6},{8,9},{9,8},{10,11... | collective-permute-start | bytes 196616 | tf_op jit(solution)/shard_map/ppermute | solution.py:314
  3.7 2.6 %collective-permute-start.1 = (f32[64,256]{1,0:T(8,128)}, f32[64,256]{1,0:T(8,128)S(1)}, u32[]{:S(2)}, u32[]{:S(2)}) collective-permute-start(f32[64,256]{1,0:T(8,128)} %panel_hbm.1), channel_id=1, source_target_pairs={{0,2},{1,3},{2,0},{3,1},{4,6},{5,7},{6,4},{7,5},{8,10},{9,11},{10,... | collective-permute-start | bytes 196616 | tf_op jit(solution)/shard_map/ppermute | solution.py:314
  6.3 0.0 collective-permute-start.2
  6.3 1.1 %stage.1 = (f32[64,256]{1,0:T(8,128)S(1)}, f32[256,512]{1,0:T(8,128)S(1)}) custom-call(f32[64,256]{1,0:T(8,128)} %panel_hbm.1, f32[256,512]{1,0:T(8,128)} %trailing_hbm.1), custom_call_target="tpu_custom_call" | custom-call | tf_op jit(solution)/shard_map/stage/pallas_call | solution.py:320
  7.5 3.8 %collective-permute-done.1.refs_2_ = f32[64,256]{1,0:T(8,128)S(1)} collective-permute-done((f32[64,256]{1,0:T(8,128)}, f32[64,256]{1,0:T(8,128)S(1)}, u32[]{:S(2)}, u32[]{:S(2)}) %collective-permute-start.1) | collective-permute-done | bytes 65568 | tf_op jit(solution)/shard_map/ppermute | solution.py:314
  11.2 1.4 %collective-permute-done.2.refs_3_ = f32[64,256]{1,0:T(8,128)S(1)} collective-permute-done((f32[64,256]{1,0:T(8,128)}, f32[64,256]{1,0:T(8,128)S(1)}, u32[]{:S(2)}, u32[]{:S(2)}) %collective-permute-start.2) | collective-permute-done | bytes 65568 | tf_op jit(solution)/shard_map/ppermute | solution.py:314
  12.6 0.3 shard_map.49
  13.0 0.4 shard_map.50
  13.4 0.1 collective-permute-start.7
  13.5 1.5 %collective-permute-done.7 = f32[256,256]{1,0:T(8,128)S(1)} collective-permute-done((f32[256,256]{1,0:T(8,128)S(1)}, f32[256,256]{1,0:T(8,128)S(1)}, u32[]{:S(2)}, u32[]{:S(2)}) %collective-permute-start.7) | collective-permute-done | bytes 262176 | tf_op jit(solution)/shard_map/ppermute | solution.py:314
  15.1 1.6 %collective-permute-start.8 = (f32[256,256]{1,0:T(8,128)S(1)}, f32[256,256]{1,0:T(8,128)S(1)}, u32[]{:S(2)}, u32[]{:S(2)}) collective-permute-start(f32[256,256]{1,0:T(8,128)S(1)} %add.21), channel_id=1, source_target_pairs={{0,8},{4,20},{8,0},{12,28},{16,24},{20,4},{24,16},{28,12},{1,9},{5... | collective-permute-start | bytes 786440 | tf_op jit(solution)/shard_map/ppermute | solution.py:314
  16.6 4.9 %collective-permute-done.8 = f32[256,256]{1,0:T(8,128)S(1)} collective-permute-done((f32[256,256]{1,0:T(8,128)S(1)}, f32[256,256]{1,0:T(8,128)S(1)}, u32[]{:S(2)}, u32[]{:S(2)}) %collective-permute-start.8) | collective-permute-done | bytes 262176 | tf_op jit(solution)/shard_map/ppermute | solution.py:314
  21.5 1.6 %collective-permute-start.9 = (f32[256,256]{1,0:T(8,128)S(1)}, f32[256,256]{1,0:T(8,128)S(1)}, u32[]{:S(2)}, u32[]{:S(2)}) collective-permute-start(f32[256,256]{1,0:T(8,128)S(1)} %add.22), channel_id=1, source_target_pairs={{0,16},{4,12},{8,24},{12,4},{16,0},{20,28},{24,8},{28,20},{1,17},{... | collective-permute-start | bytes 786440 | tf_op jit(solution)/shard_map/ppermute | solution.py:314
  23.1 4.8 %collective-permute-done.9 = f32[256,256]{1,0:T(8,128)S(1)} collective-permute-done((f32[256,256]{1,0:T(8,128)S(1)}, f32[256,256]{1,0:T(8,128)S(1)}, u32[]{:S(2)}, u32[]{:S(2)}) %collective-permute-start.9) | collective-permute-done | bytes 262176 | tf_op jit(solution)/shard_map/ppermute | solution.py:314
  28.0 0.1 collective-permute-start.10
  28.1 1.6 %collective-permute-start.4 = (f32[136,128]{1,0:T(8,128)S(1)}, f32[136,128]{1,0:T(8,128)S(1)}, u32[]{:S(2)}, u32[]{:S(2)}) collective-permute-start(f32[136,128]{1,0:T(8,128)S(1)} %add.18), channel_id=1, source_target_pairs={{0,8},{4,20},{8,0},{12,28},{16,24},{20,4},{24,16},{28,12},{1,9},{5... | collective-permute-start | bytes 208904 | tf_op jit(solution)/shard_map/ppermute | solution.py:314
  29.7 2.8 %collective-permute-done.4 = f32[136,128]{1,0:T(8,128)S(1)} collective-permute-done((f32[136,128]{1,0:T(8,128)S(1)}, f32[136,128]{1,0:T(8,128)S(1)}, u32[]{:S(2)}, u32[]{:S(2)}) %collective-permute-start.4) | collective-permute-done | bytes 69664 | tf_op jit(solution)/shard_map/ppermute | solution.py:314
  32.5 1.6 %collective-permute-start.5 = (f32[136,128]{1,0:T(8,128)S(1)}, f32[136,128]{1,0:T(8,128)S(1)}, u32[]{:S(2)}, u32[]{:S(2)}) collective-permute-start(f32[136,128]{1,0:T(8,128)S(1)} %add.19), channel_id=1, source_target_pairs={{0,16},{4,12},{8,24},{12,4},{16,0},{20,28},{24,8},{28,20},{1,17},{... | collective-permute-start | bytes 208904 | tf_op jit(solution)/shard_map/ppermute | solution.py:314
  34.1 2.8 %collective-permute-done.5 = f32[136,128]{1,0:T(8,128)S(1)} collective-permute-done((f32[136,128]{1,0:T(8,128)S(1)}, f32[136,128]{1,0:T(8,128)S(1)}, u32[]{:S(2)}, u32[]{:S(2)}) %collective-permute-start.5) | collective-permute-done | bytes 69664 | tf_op jit(solution)/shard_map/ppermute | solution.py:314
  36.9 0.1 collective-permute-start.6
  37.0 1.2 %collective-permute-done.6.other_ref = f32[136,128]{1,0:T(8,128)S(1)} collective-permute-done((f32[136,128]{1,0:T(8,128)S(1)}, f32[136,128]{1,0:T(8,128)S(1)}, u32[]{:S(2)}, u32[]{:S(2)}) %collective-permute-start.6) | collective-permute-done | bytes 69664 | tf_op jit(solution)/shard_map/ppermute | solution.py:314
  38.2 5.2 %factor_first.1 = (f32[256,256]{1,0:T(8,128)S(1)}, f32[256,256]{1,0:T(8,128)S(1)}, f32[256,256]{1,0:T(8,128)S(1)}, f32[256,128]{1,0:T(8,128)S(1)}, f32[256,256]{1,0:T(8,128)}) custom-call(f32[136,128]{1,0:T(8,128)S(1)} %add.20.mine_ref, f32[136,128]{1,0:T(8,128)S(1)} %collective-permute-done.6.other_ref, f32[256,256]{1,0:T(8,128)S(1)} %get-tuple-element.24.panel_ref), custom_call_target="tpu_custom_call" | custom-call | tf_op jit(solution)/shard_map/factor_first/pallas_call | solution.py:352
  43.4 1.1 %shard_map.51 = (f32[256,256]{1,0:T(8,128)S(1)}, f32[256,256]{1,0:T(8,128)S(1)}, f32[256,256]{1,0:T(8,128)S(1)}, bf16[128,384]{1,0:T(8,128)(2,1)S(1)}, bf16[128,...) custom-call(f32[256,256]{1,0:T(8,128)S(1)} %get-tuple-element.25.m0_, ...), custom_call_target="tpu_custom_call", output_to_operand_aliasing={{0}: (0, {}), {1}: (1, {}), {2}: (2, {})} | custom-call | tf_op jit(solution)/shard_map/pallas_call | solution.py:37
  44.5 1.4 %finish.1 = (f32[256,256]{1,0:T(8,128)}, f32[256,512]{1,0:T(8,128)}, f32[256,512]{1,0:T(8,128)}) custom-call(f32[256,256]{1,0:T(8,128)S(1)} %get-tuple-element.32.refs_0_, bf16[128,384]{1,0:T(8,128)(2,1)S(1)} %get-tuple-element.33.refs_1_, bf16[128,768]{1,0:T(8,128)(2,1)S(1)} %get-tuple-element.34.refs_2_, ...), custom_call_target="tpu_custom_call", output_to_operand_aliasing={{0}: (8, {})} | custom-call | tf_op jit(solution)/shard_map/finish/pallas_call | solution.py:376
  (10 shorter events, 0.1 us)
Async XLA Ops:
  0.6 6.8 %collective-permute-start = (f32[64,256]{1,0:T(8,128)}, f32[64,256]{1,0:T(8,128)S(1)}, u32[]{:S(2)}, u32[]{:S(2)}) collective-permute-start(f32[64,256]{1,0:T(8,128)} %panel_hbm.1), channel_id=1, source_target_pairs={{0,1},{1,0},{2,3},{3,2},{4,5},{5,4},{6,7},{7,6},{8,9},{9,8},{10,11... | collective-permute-start | bytes 196616 | tf_op jit(solution)/shard_map/ppermute | solution.py:314
  3.7 7.5 %collective-permute-start.1 = (f32[64,256]{1,0:T(8,128)}, f32[64,256]{1,0:T(8,128)S(1)}, u32[]{:S(2)}, u32[]{:S(2)}) collective-permute-start(f32[64,256]{1,0:T(8,128)} %panel_hbm.1), channel_id=1, source_target_pairs={{0,2},{1,3},{2,0},{3,1},{4,6},{5,7},{6,4},{7,5},{8,10},{9,11},{10,... | collective-permute-start | bytes 196616 | tf_op jit(solution)/shard_map/ppermute | solution.py:314
  6.3 6.3 %collective-permute-start.2 = (f32[64,256]{1,0:T(8,128)}, f32[64,256]{1,0:T(8,128)S(1)}, u32[]{:S(2)}, u32[]{:S(2)}) collective-permute-start(f32[64,256]{1,0:T(8,128)} %panel_hbm.1), channel_id=1, source_target_pairs={{0,3},{1,2},{2,1},{3,0},{4,7},{5,6},{6,5},{7,4},{8,11},{9,10},{10,... | collective-permute-start | bytes 196616 | tf_op jit(solution)/shard_map/ppermute | solution.py:314
  13.4 1.6 %collective-permute-start.7 = (f32[256,256]{1,0:T(8,128)S(1)}, f32[256,256]{1,0:T(8,128)S(1)}, u32[]{:S(2)}, u32[]{:S(2)}) collective-permute-start(f32[256,256]{1,0:T(8,128)S(1)} %get-tuple-element.31), channel_id=1, source_target_pairs={{0,4},{4,0},{8,12},{12,8},{16,20},{20,16},{24,28},{28,24},{1,5},{5... | collective-permute-start | bytes 786440 | tf_op jit(solution)/shard_map/ppermute | solution.py:314
  15.1 6.4 %collective-permute-start.8 = (f32[256,256]{1,0:T(8,128)S(1)}, f32[256,256]{1,0:T(8,128)S(1)}, u32[]{:S(2)}, u32[]{:S(2)}) collective-permute-start(f32[256,256]{1,0:T(8,128)S(1)} %add.21), channel_id=1, source_target_pairs={{0,8},{4,20},{8,0},{12,28},{16,24},{20,4},{24,16},{28,12},{1,9},{5... | collective-permute-start | bytes 786440 | tf_op jit(solution)/shard_map/ppermute | solution.py:314
  21.5 6.4 %collective-permute-start.9 = (f32[256,256]{1,0:T(8,128)S(1)}, f32[256,256]{1,0:T(8,128)S(1)}, u32[]{:S(2)}, u32[]{:S(2)}) collective-permute-start(f32[256,256]{1,0:T(8,128)S(1)} %add.22), channel_id=1, source_target_pairs={{0,16},{4,12},{8,24},{12,4},{16,0},{20,28},{24,8},{28,20},{1,17},{... | collective-permute-start | bytes 786440 | tf_op jit(solution)/shard_map/ppermute | solution.py:314
  23.1 5.0 %collective-permute-start.3 = (f32[136,128]{1,0:T(8,128)S(1)}, f32[136,128]{1,0:T(8,128)S(1)}, u32[]{:S(2)}, u32[]{:S(2)}) collective-permute-start(f32[136,128]{1,0:T(8,128)S(1)} %get-tuple-element.23), channel_id=1, source_target_pairs={{0,4},{4,0},{8,12},{12,8},{16,20},{20,16},{24,28},{28,24},{1,5},{5... | collective-permute-start | bytes 208904 | tf_op jit(solution)/shard_map/ppermute | solution.py:314
  28.0 16.5 %collective-permute-start.10 = (f32[256,256]{1,0:T(8,128)S(1)}, f32[256,256]{1,0:T(8,128)S(1)}, u32[]{:S(2)}, u32[]{:S(2)}) collective-permute-start(f32[256,256]{1,0:T(8,128)S(1)} %add.23.terms_ref), channel_id=1, source_target_pairs={{0,4},{4,0},{8,12},{12,8},{16,20},{20,16},{24,28},{28,24},{1,5},{5... | collective-permute-start | bytes 786440 | tf_op jit(solution)/shard_map/ppermute | solution.py:314
  28.1 4.4 %collective-permute-start.4 = (f32[136,128]{1,0:T(8,128)S(1)}, f32[136,128]{1,0:T(8,128)S(1)}, u32[]{:S(2)}, u32[]{:S(2)}) collective-permute-start(f32[136,128]{1,0:T(8,128)S(1)} %add.18), channel_id=1, source_target_pairs={{0,8},{4,20},{8,0},{12,28},{16,24},{20,4},{24,16},{28,12},{1,9},{5... | collective-permute-start | bytes 208904 | tf_op jit(solution)/shard_map/ppermute | solution.py:314
  32.5 4.4 %collective-permute-start.5 = (f32[136,128]{1,0:T(8,128)S(1)}, f32[136,128]{1,0:T(8,128)S(1)}, u32[]{:S(2)}, u32[]{:S(2)}) collective-permute-start(f32[136,128]{1,0:T(8,128)S(1)} %add.19), channel_id=1, source_target_pairs={{0,16},{4,12},{8,24},{12,4},{16,0},{20,28},{24,8},{28,20},{1,17},{... | collective-permute-start | bytes 208904 | tf_op jit(solution)/shard_map/ppermute | solution.py:314
  36.9 1.3 %collective-permute-start.6 = (f32[136,128]{1,0:T(8,128)S(1)}, f32[136,128]{1,0:T(8,128)S(1)}, u32[]{:S(2)}, u32[]{:S(2)}) collective-permute-start(f32[136,128]{1,0:T(8,128)S(1)} %add.20.mine_ref), channel_id=1, source_target_pairs={{0,4},{4,0},{8,12},{12,8},{16,20},{20,16},{24,28},{28,24},{1,5},{5... | collective-permute-start | bytes 208904 | tf_op jit(solution)/shard_map/ppermute | solution.py:314
